TPU v7x, 256 devices: a whole 4x4x8 slice. The times are simulated.
256 devices in a mesh: gx: 4 (over y), gy: 8 (over x, core), gz: 8 (over z).
Axes of the slice: x: 4, y: 4, z: 8, core: 2. Of those that a mesh axis runs over, the one named last changes fastest.
Arguments:
- field: float32 [4, 16384, 512], P(None, ('gx', 'gy', 'gz')), may hold values from -6 to 6
- neighbours: int32 [16384, 6], P(('gx', 'gy', 'gz')), may hold values from -1 to 16383, as said below
- cell_one: int32 [524288], P(('gx', 'gy', 'gz')), may hold values from 0 to 16383, as said below
- ref_one: float32 [3, 524288], P(None, ('gx', 'gy', 'gz')), may hold values from -1 to 1
- cell_two: int32 [524288], P(('gx', 'gy', 'gz')), may hold values from 0 to 16383, as said below
- ref_two: float32 [3, 524288], P(None, ('gx', 'gy', 'gz')), may hold values from -1 to 1
- velocity: float32 [3, 524288], P(None, ('gx', 'gy', 'gz')), may hold values from -6 to 6
- rate: float32 [524288], P(('gx', 'gy', 'gz')), may hold values from 0.5 to 8
- cut: int32 [1], replicated, may hold values from 1 to 2047
Outputs:
- field_out: float32 [4, 16384, 512], P(None, ('gx', 'gy', 'gz'))
- velocity_out: float32 [3, 524288], P(None, ('gx', 'gy', 'gz'))
Inputs may be any that keep to these rules, and one draw needn't show every extreme that they name: `neighbours`: across face f of an element lies an element of the same device or of the adjacent device along that face's axis (cyclic along gz), with the same face node order; -1 marks walls at the ends along gx and gy. The order of elements within a device is arbitrary. `cell_one`: A particle's element is owned by a device with the same gx index as its bin. From one bin at most 64 particles lie in the elements of one device, and in each slab one device receives exactly 64 from every bin of the slab. `cell_two`: as for cell_one, for the second step's bins.
All inputs are finite; a program needn't handle non-finite values.
Results may differ from a plain program's by a relative error of at most 0.0003.
Values sent between devices are 32-bit elements; how exact they have to be, the bound alone decides.
No kernel may reach another device: no remote copies, remote signals or barrier semaphores. Data moves between devices by JAX's collectives and lax.ppermute only.
A program may use at most 128 MiB of HBM per device.

v0:
```python
import functools

import jax
import jax.numpy as jnp
import numpy as np
from jax import lax
from jax.experimental import pallas as pl
from jax.experimental.pallas import tpu as pltpu
from jax.sharding import PartitionSpec as P


node_points = -np.cos(np.pi * np.arange(8) / 7.0)
step_time = 0.1
viscosity = 0.002
penalty = 0.25
loading = 0.5
heating = 0.5

ELEMS = 64
OWNERS = 64
BIN = 2048
CAP = 64
ROWS = OWNERS * CAP // 128
CHUNK_ROWS = 4
CHUNK = 128 * CHUNK_ROWS
BODY = 8

f32 = jnp.float32
bf16 = jnp.bfloat16
i32 = jnp.int32


def laplace_table():
    differences = node_points[:, None] - node_points[None, :] + np.eye(8)
    weights = 1.0 / np.prod(differences, axis=1)
    derivative = weights[None, :] / weights[:, None] / differences
    derivative = derivative * (1.0 - np.eye(8))
    derivative = derivative - np.eye(8) * derivative.sum(axis=1)[:, None]
    second = derivative @ derivative
    identity = np.eye(8)
    operator = np.kron(np.kron(second, identity), identity)
    operator = operator + np.kron(np.kron(identity, second), identity)
    operator = operator + np.kron(np.kron(identity, identity), second)
    return operator.T


def face_table():
    selection = np.zeros((512, 384))
    for face_side in range(6):
        edge_value = 0 if face_side % 2 == 0 else 7
        for row_node in range(8):
            for col_node in range(8):
                if face_side < 2:
                    node_index = (edge_value * 8 + row_node) * 8 + col_node
                elif face_side < 4:
                    node_index = (row_node * 8 + edge_value) * 8 + col_node
                else:
                    node_index = (row_node * 8 + col_node) * 8 + edge_value
                selection[node_index, face_side * 64 + row_node * 8 + col_node] = 1.0
    return selection


def face_select():
    col = iota((1, 384), 1)
    side, first, second = col >> 6, (col >> 3) & 7, col & 7
    edge = (side & 1) * 7
    node_a = edge * 64 + first * 8 + second
    node_b = first * 64 + edge * 8 + second
    node_c = first * 64 + second * 8 + edge
    node = jnp.where(side < 2, node_a, jnp.where(side < 4, node_b, node_c))
    return jnp.where(iota((512, 384), 0) == node, 1.0, 0.0).astype(bf16)


def iota(shape, axis):
    return lax.broadcasted_iota(i32, shape, axis)


def split(x):
    high = x.astype(bf16)
    return high, (x - high.astype(f32)).astype(bf16)


def split_row(x):
    high = x.astype(bf16).astype(f32)
    return high, x - high


def dot(a, b):
    return jnp.dot(a, b, preferred_element_type=f32)


def dot_nt(a, b):
    return lax.dot_general(a, b, (((1,), (1,)), ((), ())), preferred_element_type=f32)


def rank_in_owner(owner):
    width = 256
    upto = jnp.where(iota((width, width), 0) <= iota((width, width), 1), 1.0, 0.0).astype(bf16)
    table = jnp.concatenate([upto, jnp.ones((width, width), bf16)], axis=0)
    before = jnp.zeros((OWNERS, width), f32)
    ranks = []
    for start in range(0, BIN, width):
        here = iota((OWNERS, width), 0) == owner[:, start : start + width]
        marks = jnp.where(here, 1.0, 0.0)
        counts = dot(jnp.concatenate([marks, before], axis=1).astype(bf16), table)
        ranks.append(jnp.sum(jnp.where(here, counts, 0.0), axis=0, keepdims=True) - 1.0)
        before = before + marks
    return jnp.concatenate(ranks, axis=1)


def thick(row, rows):
    sixteen = jnp.broadcast_to(row, (16, row.shape[1])).astype(bf16)
    return jnp.concatenate([sixteen] * (rows // 16), axis=0)


def one_hot(index, rows):
    return jnp.where(iota((rows, index.shape[1]), 0) == index, 1.0, 0.0).astype(bf16)


def scatter_slots(out_ref, owner, rank, values):
    owned = one_hot(owner, OWNERS)
    placed = one_hot(rank, CAP)
    for first in range(0, len(values), 4):
        highs, lows = [], []
        for value in values[first : first + 4]:
            high, low = split_row(value)
            highs.append(placed * thick(high, CAP))
            lows.append(placed * thick(low, CAP))
        out = dot_nt(owned, jnp.concatenate(highs, axis=0)) + dot_nt(
            owned, jnp.concatenate(lows, axis=0)
        )
        out_ref[:, first // 2, :] = out[:, :128]
        out_ref[:, first // 2 + 1, :] = out[:, 128:]


def gather_slots(blocks, owner, lane_hot):
    high, low = split(jnp.concatenate(blocks, axis=0))
    total = dot(jnp.concatenate([high, low], axis=1), jnp.concatenate([lane_hot] * 2, axis=0))
    owned = iota((OWNERS, BIN), 0) == owner
    return [
        jnp.sum(jnp.where(owned, total[k * OWNERS : (k + 1) * OWNERS], 0.0), axis=0, keepdims=True)
        for k in range(len(blocks))
    ]


def send_kernel(cell_ref, coord_ref, speed_ref, rate_ref, out_ref, code_ref):
    cell = cell_ref[...]
    owner = (cell >> 6) & (OWNERS - 1)
    element = (cell & (ELEMS - 1)).astype(f32)
    rank = rank_in_owner(owner)
    code_ref[0:1, :] = owner.astype(f32) * float(CAP) + rank
    code_ref[1:2, :] = rate_ref[...]
    values = [
        element,
        speed_ref[0:1, :],
        coord_ref[0:1, :],
        speed_ref[1:2, :],
        coord_ref[1:2, :],
        speed_ref[2:3, :],
        coord_ref[2:3, :],
        rate_ref[...],
    ]
    scatter_slots(out_ref, owner, rank.astype(i32), values)


def resend_kernel(cut_ref, back_ref, moved_ref, cell_ref, code_ref, coord_ref, out_ref):
    first_code = moved_ref[0:1, :].astype(i32)
    rate = moved_ref[1:2, :]
    part = jnp.where(iota((1, BIN), 1) + cut_ref[0] >= BIN, CAP, 0)
    lane_hot = one_hot((first_code & (CAP - 1)) + part, 128)
    speeds = gather_slots([back_ref[:, k, :] for k in range(3)], first_code >> 6, lane_hot)
    element = (cell_ref[...] & (ELEMS - 1)).astype(f32)
    code = code_ref[...]
    values = [
        element,
        speeds[0],
        coord_ref[0:1, :],
        speeds[1],
        coord_ref[1:2, :],
        speeds[2],
        coord_ref[2:3, :],
        rate,
    ]
    scatter_slots(out_ref, code >> 6, code & (CAP - 1), values)


def final_kernel(back_ref, code_ref, out_ref):
    code = code_ref[...]
    lane_hot = jnp.concatenate([one_hot(code & (CAP - 1), CAP)] * 2, axis=0)
    left = iota((OWNERS, 128), 1) < 64
    pair, last = back_ref[:, 0, :], back_ref[:, 1, :]
    blocks = [jnp.where(left, pair, 0.0), jnp.where(left, 0.0, pair), jnp.where(left, last, 0.0)]
    speeds = gather_slots(blocks, code >> 6, lane_hot)
    for k in range(3):
        out_ref[k : k + 1, :] = speeds[k]


def column(values):
    row = iota((8, 1), 0)
    result = jnp.zeros((8, 1), f32)
    for index, value in enumerate(values):
        result = jnp.where(row == index, float(value), result)
    return result


def lagrange(x):
    gaps = node_points[:, None] - node_points[None, :] + np.eye(8)
    one = pltpu.roll(x - column(node_points), 1, 0)
    two = one * pltpu.roll(one, 1, 0)
    four = two * pltpu.roll(two, 2, 0)
    last = pltpu.roll(one, 6, 0) * column(1.0 / np.prod(gaps, axis=1))
    return four * pltpu.roll(two, 4, 0) * last


def basis(coords, pair_ref, weight_ref):
    first, second, third = [lagrange(x) for x in coords]
    for a in range(8):
        pair_ref[8 * a : 8 * a + 8, :] = first[a : a + 1, :] * second
    for i in range(32):
        piece = jnp.concatenate(
            [pair_ref[2 * i + h : 2 * i + h + 1, :] * third for h in range(2)], axis=0
        )
        weight_ref[16 * i : 16 * i + 16, :], weight_ref[512 + 16 * i : 528 + 16 * i, :] = split(piece)


def along(rows, k):
    return jnp.concatenate([rows[i, k : k + 1, :] for i in range(CHUNK_ROWS)], axis=1)


def particle_kernel(shift, incoming_ref, state_ref, back_ref, force_ref, even_ref, odd_ref, fresh_ref, state_scr, pair_refs, weight_refs, source_refs, total_ref):
    low, high = incoming_ref[0:ROWS], incoming_ref[ROWS : 2 * ROWS]
    left = iota(low.shape, 2) < 64
    even_ref[...] = jnp.where(left, low, pltpu.roll(high, 64, 2))
    odd_ref[...] = jnp.where(left, pltpu.roll(low, 64, 2), high)
    high, low = split(state_ref[0:3].reshape(3 * ELEMS, 512))
    state_scr[0 : 3 * ELEMS] = high
    state_scr[3 * ELEMS :] = low
    fresh_ref[:, 3:4, :] = jnp.zeros((ROWS + 1, 1, 128), f32)

    total_ref[...] = jnp.zeros_like(total_ref)

    def one(start, weight_ref, source_ref, pair_ref):
        even = even_ref[pl.ds(start, CHUNK_ROWS)]
        odd = odd_ref[pl.ds(start, CHUNK_ROWS)]
        basis([along(even, k) for k in (1, 2, 3)], pair_ref, weight_ref)
        wide = dot(state_scr[...], weight_ref[0:512])
        rest = dot(state_scr[0 : 3 * ELEMS], weight_ref[512:1024])
        element = along(even, 0).astype(i32)
        here = iota((ELEMS, CHUNK), 0) == element
        rates = along(odd, 3)
        squares = None
        fresh, sources = [], []
        for k in range(3):
            rows = slice(k * ELEMS, (k + 1) * ELEMS)
            lower = slice((k + 3) * ELEMS, (k + 4) * ELEMS)
            picked = jnp.where(here, wide[rows] + wide[lower] + rest[rows], 0.0)
            speed = along(odd, k)
            offset = jnp.sum(picked, axis=0, keepdims=True) - speed
            accel = rates * offset
            squares = offset * offset if squares is None else squares + offset * offset
            sources.append(accel)
            fresh.append(speed + step_time * accel)
        sources.append(rates * squares)
        for i in range(CHUNK_ROWS):
            for k in range(3):
                fresh_ref[start + i, k : k + 1, :] = fresh[k][:, i * 128 : (i + 1) * 128]
        hot = one_hot(element, ELEMS)
        for k in range(4):
            high, low = split_row(sources[k])
            source_ref[0, k * ELEMS : (k + 1) * ELEMS] = hot * thick(high, ELEMS)
            source_ref[1, k * ELEMS : (k + 1) * ELEMS] = hot * thick(low, ELEMS)

    def push(weight_ref, source_ref):
        wide = dot_nt(weight_ref[...], source_ref[0])
        total_ref[...] += wide[:512] + wide[512:] + dot_nt(weight_ref[0:512], source_ref[1])

    def visit(index, carry):
        for h in range(BODY):
            one((index * BODY + h) * CHUNK_ROWS, weight_refs.at[h], source_refs.at[h], pair_refs.at[h])
        for h in range(BODY):
            push(weight_refs.at[h], source_refs.at[h])
        return carry

    lax.fori_loop(0, ROWS // CHUNK_ROWS // BODY, visit, 0)
    fresh = fresh_ref[0:ROWS]
    if shift:
        fresh_ref[ROWS] = pltpu.roll(fresh_ref[0], 64, 1)
        after = fresh_ref[1 : ROWS + 1]
        left = iota(fresh.shape, 2) < 64
        back_ref[0:ROWS] = jnp.where(left, fresh, pltpu.roll(after, 64, 2))
        back_ref[ROWS : 2 * ROWS] = jnp.where(left, pltpu.roll(fresh, 64, 2), after)
    else:
        turned = pltpu.roll(fresh, 64, 2)
        left = iota((ROWS, 1, 128), 2) < 64
        back_ref[0:ROWS, 0:1, :] = jnp.where(left, fresh[:, 0:1, :], turned[:, 1:2, :])
        back_ref[0:ROWS, 1:2, :] = fresh[:, 2:3, :]
        back_ref[ROWS : 2 * ROWS, 0:1, :] = jnp.where(left, turned[:, 0:1, :], fresh[:, 1:2, :])
        back_ref[ROWS : 2 * ROWS, 1:2, :] = turned[:, 2:3, :]
    force_ref[...] = total_ref[...].T


def pick_faces(state, select, chosen_ref, faces_ref, send_refs):
    high, low = split(state)
    picked = dot(jnp.concatenate([high, low], axis=0), select)
    picked = picked[: 4 * ELEMS] + picked[4 * ELEMS :]
    left = iota((ELEMS, 128), 1) < 64
    for pair in range(3):
        tiles = [picked[k * ELEMS : (k + 1) * ELEMS, pair * 128 : (pair + 1) * 128] for k in range(4)]
        turned = [pltpu.roll(tile, 64, 1) for tile in tiles]
        lower = [jnp.where(left, tiles[k], turned[k + 1]) for k in (0, 2)]
        upper = [jnp.where(left, turned[k], tiles[k + 1]) for k in (0, 2)]
        for side, parts in ((2 * pair, lower), (2 * pair + 1, upper)):
            face = jnp.concatenate(parts, axis=1)
            faces_ref[side] = face
            face_high, face_low = split(face)
            send_refs[side][...] = dot(chosen_ref[side], face_high) + dot(chosen_ref[side], face_low)


def links_kernel(device_ref, state_ref, near_t_ref, chosen_ref, faces_ref, *send_refs):
    device = device_ref[0]
    near_t = near_t_ref[...].astype(f32)
    near = jnp.concatenate([near_t, near_t[0:2]], axis=0).T.astype(i32)
    for side in range(6):
        outside = (near[:, side : side + 1] >> 6) != device
        outside_t = (near_t_ref[side : side + 1, :] >> 6) != device
        before = (iota((ELEMS, ELEMS), 0) < iota((ELEMS, ELEMS), 1)) & outside
        rank = jnp.sum(jnp.where(before, 1.0, 0.0), axis=0, keepdims=True)
        rank = jnp.where(outside_t, rank, -1.0)
        chosen = iota((16, ELEMS), 0).astype(f32) == rank
        chosen_ref[side] = jnp.where(chosen, 1.0, 0.0).astype(bf16)
    pick_faces(state_ref[...].reshape(4 * ELEMS, 512), face_select(), chosen_ref, faces_ref, send_refs)


def tables_kernel(device_ref, near_t_ref, cell_ref, code_ref, own_ref, far_ref):
    device = device_ref[0]
    near_t = near_t_ref[...].astype(f32)
    near = jnp.concatenate([near_t, near_t[0:2]], axis=0).T.astype(i32)
    for side in range(6):
        target = near[:, side : side + 1]
        target_t = near_t_ref[side : side + 1, :]
        outside = (target >> 6) != device
        remote = (target >= 0) & outside
        remote_t = (target_t >= 0) & ((target_t >> 6) != device)
        slot = jnp.where(outside, -1, target & (ELEMS - 1))
        own = (iota((ELEMS, 2 * ELEMS), 1) & (ELEMS - 1)) == slot
        own_ref[side] = jnp.where(own, 1.0, 0.0).astype(bf16)
        key = jnp.where(remote, target & (ELEMS - 1), ELEMS)
        key_t = jnp.where(remote_t, target_t & (ELEMS - 1), ELEMS)
        rank = jnp.sum(jnp.where(key_t < key, 1.0, 0.0), axis=1, keepdims=True)
        rank = jnp.where(remote, rank, -1.0)
        far = (iota((ELEMS, 32), 1) & 15).astype(f32) == rank
        far_ref[side] = jnp.where(far, 1.0, 0.0).astype(bf16)
    owner = (cell_ref[...] >> 6) & (OWNERS - 1)
    code_ref[...] = owner * CAP + rank_in_owner(owner).astype(i32)


def fluid_kernel(again, state_ref, force_ref, own_ref, far_ref, lap_high_ref, lap_low_ref, keep_ref, faces_ref, *refs):
    halo_refs, refs = refs[:6], refs[6:]
    if again:
        chosen_ref, out_ref, next_ref = refs[:3]
        send_refs = refs[3:]
    else:
        (out_ref,) = refs
    partners = []
    for side in range(6):
        face = jnp.concatenate(split(faces_ref[side ^ 1]), axis=0)
        halo = jnp.concatenate(split(halo_refs[side][...]), axis=0)
        partners.append(dot(own_ref[side], face) + dot(far_ref[side], halo))
    left = iota((ELEMS, 128), 1) < 64
    turned = [[pltpu.roll(p[:, h * 128 : (h + 1) * 128], 64, 1) for h in range(2)] for p in partners]
    joined = []
    for k in range(4):
        h = k // 2
        row = []
        for pair in range(3):
            lower, upper = partners[2 * pair], partners[2 * pair + 1]
            lanes = slice(h * 128, (h + 1) * 128)
            if k % 2 == 0:
                row.append(jnp.where(left, lower[:, lanes], turned[2 * pair + 1][h]))
            else:
                row.append(jnp.where(left, turned[2 * pair][h], upper[:, lanes]))
        joined.append(jnp.concatenate(row, axis=1))
    high, low = split(jnp.concatenate(joined, axis=0))
    select = face_select()
    spread = dot_nt(jnp.concatenate([high, low], axis=0), select)
    spread = spread[: 4 * ELEMS] + spread[4 * ELEMS :]
    state = state_ref[...].reshape(4 * ELEMS, 512)
    high, low = split(state)
    wide = dot(jnp.concatenate([high, low], axis=0), lap_high_ref[...])
    laplace = wide[: 4 * ELEMS] + wide[4 * ELEMS :] + dot(high, lap_low_ref[...])
    result = state * keep_ref[...] + viscosity * laplace + penalty * spread
    row = iota((4 * ELEMS, 1), 0)
    result = result + jnp.where(row < 3 * ELEMS, -loading, heating) * force_ref[...]
    out_ref[...] = result.reshape(4, ELEMS, 512)
    if again:
        pick_faces(result, select, chosen_ref, next_ref, send_refs)


def call(kernel, shapes, scratch=(), scalars=0, near=()):
    vmem = pl.BlockSpec(memory_space=pltpu.VMEM)
    smem = pl.BlockSpec(memory_space=pltpu.SMEM)

    def run(*args):
        args = list(args)
        for place in near:
            args[place] = pltpu.with_memory_space_constraint(args[place], pltpu.VMEM)
        return pl.pallas_call(
            kernel,
            out_shape=shapes,
            in_specs=[smem] * scalars + [vmem] * (len(args) - scalars),
            out_specs=jax.tree.map(lambda _: vmem, shapes),
            scratch_shapes=list(scratch),
        )(*args)

    return run


def close(*dims, dtype=f32):
    return pltpu.VMEM(dims, dtype)


def shape(*dims, dtype=f32):
    return jax.ShapeDtypeStruct(dims, dtype)


def local(field, neighbours, cell_one, ref_one, cell_two, ref_two, velocity, rate, cut):
    device = lax.axis_index(("gx", "gy", "gz")).astype(i32).reshape(1)
    near_t = neighbours.T
    lap = laplace_table()
    lap_high = jnp.asarray(lap, bf16)
    lap_low = jnp.asarray(lap - np.asarray(np.asarray(lap, bf16), np.float64), bf16)
    keep = jnp.asarray(1.0 - penalty * face_table().sum(axis=1), f32)[None]
    row_one, row_two = cell_one[None], cell_two[None]
    slots = close(OWNERS, 4, 128)

    def exchange(block):
        return lax.all_to_all(block, ("gy", "gz"), split_axis=0, concat_axis=0, tiled=True)

    def neighbour_faces(sends):
        arrived = [None] * 6
        for axis_index, axis in enumerate(("gx", "gy", "gz")):
            count = lax.axis_size(axis)
            up = [(i, (i + 1) % count) for i in range(count)]
            arrived[2 * axis_index] = lax.ppermute(sends[2 * axis_index + 1], axis, up)
            arrived[2 * axis_index + 1] = lax.ppermute(
                sends[2 * axis_index], axis, [(b, a) for a, b in up]
            )
        return arrived

    face_shapes = [close(6, ELEMS, 256)] + [close(16, 256)] * 6

    def particles(incoming, state, shift):
        back = slots if shift else close(OWNERS, 2, 128)
        return call(
            functools.partial(particle_kernel, shift),
            [back, close(4 * ELEMS, 512)],
            scratch=[
                pltpu.VMEM((ROWS, 4, 128), f32),
                pltpu.VMEM((ROWS, 4, 128), f32),
                pltpu.VMEM((ROWS + 1, 4, 128), f32),
                pltpu.VMEM((6 * ELEMS, 512), bf16),
                pltpu.VMEM((BODY, 64, CHUNK), f32),
                pltpu.VMEM((BODY, 1024, CHUNK), bf16),
                pltpu.VMEM((BODY, 2, 4 * ELEMS, CHUNK), bf16),
                pltpu.VMEM((512, 4 * ELEMS), f32),
            ],
            near=(0, 1),
        )(incoming, state)

    outgoing, code_rate = call(send_kernel, [slots, shape(2, BIN)])(
        row_one, ref_one, velocity, rate[None]
    )
    incoming = exchange(outgoing)
    owners = lax.axis_size("gy") * lax.axis_size("gz")
    following = lax.ppermute(
        code_rate, ("gy", "gz"), [((i + 1) % owners, i) for i in range(owners)]
    )
    moved = lax.dynamic_slice_in_dim(
        jnp.concatenate([code_rate, following], axis=1), cut[0], BIN, 1
    )
    chosen, faces, *sends = call(
        links_kernel, [shape(6, 16, ELEMS, dtype=bf16)] + face_shapes, scalars=1
    )(device, field, near_t)
    arrived = neighbour_faces(sends)

    incoming, moved = lax.optimization_barrier((incoming, moved))
    back, force = particles(incoming, field, True)
    returned = exchange(back)
    force, near_t, row_two = lax.optimization_barrier((force, near_t, row_two))
    hots = [close(6, ELEMS, 2 * ELEMS, dtype=bf16), close(6, ELEMS, 32, dtype=bf16)]
    code_two, own, far = call(
        tables_kernel, [close(1, BIN, dtype=i32)] + hots, scalars=1, near=(1, 2)
    )(device, near_t, row_two)
    tables = (own, far, lap_high, lap_low, keep)
    middle, faces, *sends = call(
        functools.partial(fluid_kernel, True), [close(4, ELEMS, 512)] + face_shapes, near=(1, 2, 3, 7, 8, 9, 10, 11, 12, 13)
    )(field, force, *tables, faces, *arrived, chosen)
    returned, middle, *sends = lax.optimization_barrier((returned, middle, *sends))
    arrived = neighbour_faces(sends)
    outgoing = call(resend_kernel, slots, scalars=1, near=(1, 2, 3, 4, 5))(
        cut, returned, moved, row_two, code_two, ref_two
    )
    incoming = exchange(outgoing)
    back, force = particles(incoming, middle, False)
    returned = exchange(back)
    final_state = call(
        functools.partial(fluid_kernel, False), shape(4, ELEMS, 512), near=(0, 1, 2, 3, 7, 8, 9, 10, 11, 12, 13)
    )(middle, force, *tables, faces, *arrived)
    final_speeds = call(final_kernel, shape(3, BIN), near=(0, 1))(returned, code_two)
    return (final_state, final_speeds)


def solution(mesh):
    in_specs = (
        P(None, ("gx", "gy", "gz"), None),
        P(("gx", "gy", "gz"), None),
        P(("gx", "gy", "gz")),
        P(None, ("gx", "gy", "gz")),
        P(("gx", "gy", "gz")),
        P(None, ("gx", "gy", "gz")),
        P(None, ("gx", "gy", "gz")),
        P(("gx", "gy", "gz")),
        P(),
    )
    out_specs = (P(None, ("gx", "gy", "gz"), None), P(None, ("gx", "gy", "gz")))

    return jax.shard_map(local, mesh=mesh, in_specs=in_specs, out_specs=out_specs, check_vma=False)
```

profile of v0, /device:TPU:96, one launch (start us, length us, event | category | flops | bytes accessed | tf_op | source)
XLA Modules:
  0.0 106.1 jit_solution(1417699940164336840)
XLA Ops:
  0.6 3.3 %shard_map.131 = (f32[64,4,128]{2,1,0:T(4,128)}, f32[2,2048]{1,0:T(2,128)}) custom-call(s32[1,2048]{1,0:T(1,128)} %bitcast.13, f32[3,2048]{1,0:T(4,128)} %coord_ref.2, f32[3,2048]{1,0:T(4,128)} %speed_ref.1, f32[1,2048]{1,0:T(1,128)} %bitcast.14), custom_call_target="tpu_custom_call" | custom-call | tf_op jit(solution)/shard_map/pallas_call | solution.py:407
  3.9 10.8 %all-to-all-start = ((f32[64,4,128]{2,1,0:T(4,128)}), f32[64,4,128]{2,1,0:T(4,128)S(1)}, u32[]{:S(2)}, u32[]{:S(2)}) async-start(f32[64,4,128]{2,1,0:T(4,128)} %get-tuple-element.40), calls=%async_computation | async-start | bytes 262144 | tf_op jit(solution)/shard_map/all_to_all | solution.py:437
  14.7 0.0 copy-done.4
  14.7 0.6 collective-permute-start
  16.0 5.3 %collective-permute-done = f32[2,2048]{1,0:T(2,128)S(1)} collective-permute-done((f32[2,2048]{1,0:T(2,128)S(1)}, f32[2,2048]{1,0:T(2,128)S(1)}, u32[]{:S(2)}, u32[]{:S(2)}) %collective-permute-start) | collective-permute-done | bytes 16416 | tf_op jit(solution)/shard_map/ppermute | solution.py:475
  21.4 0.1 fusion.moved_ref
  21.5 2.2 %all-to-all-done.incoming_ref = f32[64,4,128]{2,1,0:T(4,128)S(1)} async-done(((f32[64,4,128]{2,1,0:T(4,128)}), f32[64,4,128]{2,1,0:T(4,128)S(1)}, u32[]{:S(2)}, u32[]{:S(2)}) %all-to-all-start) | async-done | bytes 131104 | tf_op jit(solution)/shard_map/all_to_all | solution.py:437
  23.7 1.0 copy-done
  24.7 6.5 %shard_map.132 = (f32[64,4,128]{2,1,0:T(4,128)}, f32[256,512]{1,0:T(8,128)S(1)}) custom-call(f32[64,4,128]{2,1,0:T(4,128)S(1)} %all-to-all-done.incoming_ref, f32[4,64,512]{2,1,0:T(8,128)S(1)} %copy-done), custom_call_target="tpu_custom_call" | custom-call | tf_op jit(solution)/shard_map/pallas_call | solution.py:407
  31.2 6.6 %all-to-all-start.1 = ((f32[64,4,128]{2,1,0:T(4,128)}), f32[64,4,128]{2,1,0:T(4,128)S(1)}, u32[]{:S(2)}, u32[]{:S(2)}) async-start(f32[64,4,128]{2,1,0:T(4,128)} %get-tuple-element.43), calls=%async_computation.1 | async-start | bytes 262144 | tf_op jit(solution)/shard_map/all_to_all | solution.py:437
  37.9 2.2 %shard_map.134 = (bf16[6,16,64]{2,1,0:T(8,128)(2,1)}, f32[6,64,256]{2,1,0:T(8,128)S(1)}, f32[16,256]{1,0:T(8,128)S(1)}, f32[16,256]{1,0:T(8,128)S(1)}, f32[16,25...) custom-call(s32[1]{0:T(128)} %bitcast.5.device_ref, ...), custom_call_target="tpu_custom_call" | custom-call | tf_op jit(solution)/shard_map/pallas_call | solution.py:407
  40.1 1.6 %collective-permute-start.1 = (f32[16,256]{1,0:T(8,128)S(1)}, f32[16,256]{1,0:T(8,128)S(1)}, u32[]{:S(2)}, u32[]{:S(2)}) collective-permute-start(f32[16,256]{1,0:T(8,128)S(1)} %get-tuple-element.51), channel_id=1, source_target_pairs={{0,64},{64,128},{128,192},{192,0},{1,65},{65,129},{129,193},{193,1... | collective-permute-start | bytes 49160 | tf_op jit(solution)/shard_map/ppermute | solution.py:444
  41.7 1.7 %collective-permute-start.2 = (f32[16,256]{1,0:T(8,128)S(1)}, f32[16,256]{1,0:T(8,128)S(1)}, u32[]{:S(2)}, u32[]{:S(2)}) collective-permute-start(f32[16,256]{1,0:T(8,128)S(1)} %get-tuple-element.52), channel_id=1, source_target_pairs={{64,0},{128,64},{192,128},{0,192},{65,1},{129,65},{193,129},{1,193... | collective-permute-start | bytes 49160 | tf_op jit(solution)/shard_map/ppermute | solution.py:445
  43.3 0.0 collective-permute-start.3
  43.3 3.0 %collective-permute-start.4 = (f32[16,256]{1,0:T(8,128)S(1)}, f32[16,256]{1,0:T(8,128)S(1)}, u32[]{:S(2)}, u32[]{:S(2)}) collective-permute-start(f32[16,256]{1,0:T(8,128)S(1)} %get-tuple-element.54), channel_id=1, source_target_pairs={{8,0},{16,8},{24,16},{32,24},{40,32},{48,40},{56,48},{0,56},{9,1},... | collective-permute-start | bytes 49160 | tf_op jit(solution)/shard_map/ppermute | solution.py:445
  46.3 2.7 %collective-permute-start.5 = (f32[16,256]{1,0:T(8,128)S(1)}, f32[16,256]{1,0:T(8,128)S(1)}, u32[]{:S(2)}, u32[]{:S(2)}) collective-permute-start(f32[16,256]{1,0:T(8,128)S(1)} %get-tuple-element.55), channel_id=1, source_target_pairs={{0,1},{1,2},{2,3},{3,4},{4,5},{5,6},{6,7},{7,0},{8,9},{9,10},{10,1... | collective-permute-start | bytes 49160 | tf_op jit(solution)/shard_map/ppermute | solution.py:444
  49.0 0.0 collective-permute-done.1.refs_0_
  49.0 0.0 collective-permute-start.6
  49.0 0.0 copy-done.2
  49.0 0.0 copy-done.3
  49.0 0.8 shard_map.133
  49.8 0.0 collective-permute-done.2.refs_1_
  49.8 0.0 collective-permute-done.3.refs_2_
  49.8 0.0 collective-permute-done.4.refs_3_
  49.9 0.6 collective-permute-done.5.refs_4_
  50.4 3.5 %collective-permute-done.6.refs_5_ = f32[16,256]{1,0:T(8,128)S(1)} collective-permute-done((f32[16,256]{1,0:T(8,128)S(1)}, f32[16,256]{1,0:T(8,128)S(1)}, u32[]{:S(2)}, u32[]{:S(2)}) %collective-permute-start.6) | collective-permute-done | bytes 16416 | tf_op jit(solution)/shard_map/ppermute | solution.py:445
  53.9 3.1 %shard_map.135 = (f32[4,64,512]{2,1,0:T(8,128)S(1)}, f32[6,64,256]{2,1,0:T(8,128)S(1)}, f32[16,256]{1,0:T(8,128)S(1)}, f32[16,256]{1,0:T(8,128)S(1)}, f32[16,256...) custom-call(f32[4,64,512]{2,1,0:T(8,128)} %state_ref.5, ...), custom_call_target="tpu_custom_call" | custom-call | tf_op jit(solution)/shard_map/pallas_call | solution.py:407
  57.0 0.0 all-to-all-done.1.back_ref
  57.0 0.0 copy-done.1
  57.0 1.8 %shard_map.136 = f32[64,4,128]{2,1,0:T(4,128)S(1)} custom-call(s32[1]{0:T(128)} %copy.14.cut_ref, f32[64,4,128]{2,1,0:T(4,128)S(1)} %all-to-all-done.1.back_ref, f32[2,2048]{1,0:T(2,128)S(1)} %fusion.moved_ref, s32[1,2048]{1,0:T(1,128)S(1)} %bitcast.10, s32[1,2048]{1,0:T(1,128)S(1)} %get-tuple-element.68.code_ref, f32[3,2048]{1,0:T(4,128)S(1)} %copy-done.1), custom_call_target="tpu_custom_call" | custom-call | tf_op jit(solution)/shard_map/pallas_call | solution.py:407
  58.9 15.7 %all_to_all.20.incoming_ref = f32[64,4,128]{2,1,0:T(4,128)S(1)} all-to-all(f32[64,4,128]{2,1,0:T(4,128)S(1)} %shard_map.136), channel_id=1, replica_groups=mesh['gx'=4,'gy'=8,'gz'=8] {'gy','gz'}, dimensions={0} | all-to-all | bytes 262144 | tf_op jit(solution)/shard_map/all_to_all | solution.py:437
  74.6 6.5 %shard_map.137 = (f32[64,2,128]{2,1,0:T(2,128)}, f32[256,512]{1,0:T(8,128)S(1)}) custom-call(f32[64,4,128]{2,1,0:T(4,128)S(1)} %all_to_all.20.incoming_ref, f32[4,64,512]{2,1,0:T(8,128)S(1)} %get-tuple-element.65.state_ref), custom_call_target="tpu_custom_call" | custom-call | tf_op jit(solution)/shard_map/pallas_call | solution.py:407
  81.0 6.7 %all-to-all-start.3 = ((f32[64,2,128]{2,1,0:T(2,128)}), f32[64,2,128]{2,1,0:T(2,128)S(1)}, u32[]{:S(2)}, u32[]{:S(2)}) async-start(f32[64,2,128]{2,1,0:T(2,128)} %get-tuple-element.77), calls=%async_computation.3 | async-start | bytes 131072 | tf_op jit(solution)/shard_map/all_to_all | solution.py:437
  87.8 0.7 collective-permute-start.7
  88.4 2.9 %collective-permute-start.8 = (f32[16,256]{1,0:T(8,128)S(1)}, f32[16,256]{1,0:T(8,128)S(1)}, u32[]{:S(2)}, u32[]{:S(2)}) collective-permute-start(f32[16,256]{1,0:T(8,128)S(1)} %get-tuple-element.72), channel_id=1, source_target_pairs={{64,0},{128,64},{192,128},{0,192},{65,1},{129,65},{193,129},{1,193... | collective-permute-start | bytes 49160 | tf_op jit(solution)/shard_map/ppermute | solution.py:445
  91.3 0.0 collective-permute-start.9
  91.3 3.0 %collective-permute-start.10 = (f32[16,256]{1,0:T(8,128)S(1)}, f32[16,256]{1,0:T(8,128)S(1)}, u32[]{:S(2)}, u32[]{:S(2)}) collective-permute-start(f32[16,256]{1,0:T(8,128)S(1)} %get-tuple-element.74), channel_id=1, source_target_pairs={{8,0},{16,8},{24,16},{32,24},{40,32},{48,40},{56,48},{0,56},{9,1},... | collective-permute-start | bytes 49160 | tf_op jit(solution)/shard_map/ppermute | solution.py:445
  94.3 2.7 %collective-permute-start.11 = (f32[16,256]{1,0:T(8,128)S(1)}, f32[16,256]{1,0:T(8,128)S(1)}, u32[]{:S(2)}, u32[]{:S(2)}) collective-permute-start(f32[16,256]{1,0:T(8,128)S(1)} %get-tuple-element.75), channel_id=1, source_target_pairs={{0,1},{1,2},{2,3},{3,4},{4,5},{5,6},{6,7},{7,0},{8,9},{9,10},{10,1... | collective-permute-start | bytes 49160 | tf_op jit(solution)/shard_map/ppermute | solution.py:444
  97.0 0.0 collective-permute-done.7.refs_0_
  97.0 0.0 collective-permute-start.12
  97.0 0.0 collective-permute-done.8.refs_1_
  97.0 0.0 collective-permute-done.9.refs_2_
  97.0 0.0 collective-permute-done.10.refs_3_
  97.0 1.4 %collective-permute-done.11.refs_4_ = f32[16,256]{1,0:T(8,128)S(1)} collective-permute-done((f32[16,256]{1,0:T(8,128)S(1)}, f32[16,256]{1,0:T(8,128)S(1)}, u32[]{:S(2)}, u32[]{:S(2)}) %collective-permute-start.11) | collective-permute-done | bytes 16416 | tf_op jit(solution)/shard_map/ppermute | solution.py:444
  98.4 3.5 %collective-permute-done.12.refs_5_ = f32[16,256]{1,0:T(8,128)S(1)} collective-permute-done((f32[16,256]{1,0:T(8,128)S(1)}, f32[16,256]{1,0:T(8,128)S(1)}, u32[]{:S(2)}, u32[]{:S(2)}) %collective-permute-start.12) | collective-permute-done | bytes 16416 | tf_op jit(solution)/shard_map/ppermute | solution.py:445
  101.9 3.1 %shard_map.138 = f32[4,64,512]{2,1,0:T(8,128)} custom-call(f32[4,64,512]{2,1,0:T(8,128)S(1)} %get-tuple-element.65.state_ref, f32[256,512]{1,0:T(8,128)S(1)} %get-tuple-element.69.force_ref, bf16[6,64,128]{2,1,0:T(8,128)(2,1)S(1)} %get-tuple-element.48.own_ref, bf16[6,64,32]{2,1,0:T(8,128)(2,1)S(1)} %get-tuple-element.49.far_ref, ...), custom_call_target="tpu_custom_call" | custom-call | tf_op jit(solution)/shard_map/pallas_call | solution.py:407
  105.0 0.0 all-to-all-done.3.back_ref
  105.0 1.1 shard_map.139
  (5 shorter events, 0.0 us)
Async XLA Ops:
  3.9 10.8 %copy-start.4 = (f32[2,2048]{1,0:T(2,128)S(1)}, f32[2,2048]{1,0:T(2,128)}, u32[]{:S(2)}) copy-start(f32[2,2048]{1,0:T(2,128)} %get-tuple-element.41) | copy-start | bytes 49156
  3.9 19.8 %all-to-all-start = ((f32[64,4,128]{2,1,0:T(4,128)}), f32[64,4,128]{2,1,0:T(4,128)S(1)}, u32[]{:S(2)}, u32[]{:S(2)}) async-start(f32[64,4,128]{2,1,0:T(4,128)} %get-tuple-element.40), calls=%async_computation | async-start | bytes 262144 | tf_op jit(solution)/shard_map/all_to_all | solution.py:437
  14.7 6.6 %collective-permute-start = (f32[2,2048]{1,0:T(2,128)S(1)}, f32[2,2048]{1,0:T(2,128)S(1)}, u32[]{:S(2)}, u32[]{:S(2)}) collective-permute-start(f32[2,2048]{1,0:T(2,128)S(1)} %copy-done.4), channel_id=1, source_target_pairs={{1,0},{2,1},{3,2},{4,3},{5,4},{6,5},{7,6},{8,7},{9,8},{10,9},{11,1... | collective-permute-start | bytes 49160 | tf_op jit(solution)/shard_map/ppermute | solution.py:475
  23.7 1.0 copy-start
  31.2 25.8 %all-to-all-start.1 = ((f32[64,4,128]{2,1,0:T(4,128)}), f32[64,4,128]{2,1,0:T(4,128)S(1)}, u32[]{:S(2)}, u32[]{:S(2)}) async-start(f32[64,4,128]{2,1,0:T(4,128)} %get-tuple-element.43), calls=%async_computation.1 | async-start | bytes 262144 | tf_op jit(solution)/shard_map/all_to_all | solution.py:437
  40.1 8.9 %copy-start.2 = (s32[2048]{0:T(1024)S(1)}, s32[2048]{0:T(1024)}, u32[]{:S(2)}) copy-start(s32[2048]{0:T(1024)} %param.16) | copy-start | bytes 24580
  40.1 8.9 %collective-permute-start.1 = (f32[16,256]{1,0:T(8,128)S(1)}, f32[16,256]{1,0:T(8,128)S(1)}, u32[]{:S(2)}, u32[]{:S(2)}) collective-permute-start(f32[16,256]{1,0:T(8,128)S(1)} %get-tuple-element.51), channel_id=1, source_target_pairs={{0,64},{64,128},{128,192},{192,0},{1,65},{65,129},{129,193},{193,1... | collective-permute-start | bytes 49160 | tf_op jit(solution)/shard_map/ppermute | solution.py:444
  41.7 8.2 %collective-permute-start.2 = (f32[16,256]{1,0:T(8,128)S(1)}, f32[16,256]{1,0:T(8,128)S(1)}, u32[]{:S(2)}, u32[]{:S(2)}) collective-permute-start(f32[16,256]{1,0:T(8,128)S(1)} %get-tuple-element.52), channel_id=1, source_target_pairs={{64,0},{128,64},{192,128},{0,192},{65,1},{129,65},{193,129},{1,193... | collective-permute-start | bytes 49160 | tf_op jit(solution)/shard_map/ppermute | solution.py:445
  43.3 6.5 %collective-permute-start.3 = (f32[16,256]{1,0:T(8,128)S(1)}, f32[16,256]{1,0:T(8,128)S(1)}, u32[]{:S(2)}, u32[]{:S(2)}) collective-permute-start(f32[16,256]{1,0:T(8,128)S(1)} %get-tuple-element.53), channel_id=1, source_target_pairs={{0,8},{8,16},{16,24},{24,32},{32,40},{40,48},{48,56},{56,0},{1,9},... | collective-permute-start | bytes 49160 | tf_op jit(solution)/shard_map/ppermute | solution.py:444
  43.3 5.7 %copy-start.3 = (s32[64,6]{0,1:T(8,128)S(1)}, s32[64,6]{0,1:T(8,128)}, u32[]{:S(2)}) copy-start(s32[64,6]{0,1:T(8,128)} %param.13) | copy-start | bytes 4612
  43.3 6.5 %collective-permute-start.4 = (f32[16,256]{1,0:T(8,128)S(1)}, f32[16,256]{1,0:T(8,128)S(1)}, u32[]{:S(2)}, u32[]{:S(2)}) collective-permute-start(f32[16,256]{1,0:T(8,128)S(1)} %get-tuple-element.54), channel_id=1, source_target_pairs={{8,0},{16,8},{24,16},{32,24},{40,32},{48,40},{56,48},{0,56},{9,1},... | collective-permute-start | bytes 49160 | tf_op jit(solution)/shard_map/ppermute | solution.py:445
  46.3 4.1 %collective-permute-start.5 = (f32[16,256]{1,0:T(8,128)S(1)}, f32[16,256]{1,0:T(8,128)S(1)}, u32[]{:S(2)}, u32[]{:S(2)}) collective-permute-start(f32[16,256]{1,0:T(8,128)S(1)} %get-tuple-element.55), channel_id=1, source_target_pairs={{0,1},{1,2},{2,3},{3,4},{4,5},{5,6},{6,7},{7,0},{8,9},{9,10},{10,1... | collective-permute-start | bytes 49160 | tf_op jit(solution)/shard_map/ppermute | solution.py:444
  49.0 5.0 %collective-permute-start.6 = (f32[16,256]{1,0:T(8,128)S(1)}, f32[16,256]{1,0:T(8,128)S(1)}, u32[]{:S(2)}, u32[]{:S(2)}) collective-permute-start(f32[16,256]{1,0:T(8,128)S(1)} %get-tuple-element.56), channel_id=1, source_target_pairs={{1,0},{2,1},{3,2},{4,3},{5,4},{6,5},{7,6},{0,7},{9,8},{10,9},{11,1... | collective-permute-start | bytes 49160 | tf_op jit(solution)/shard_map/ppermute | solution.py:445
  53.9 3.1 %copy-start.1 = (f32[3,2048]{1,0:T(4,128)S(1)}, f32[3,2048]{1,0:T(4,128)}, u32[]{:S(2)}) copy-start(f32[3,2048]{1,0:T(4,128)} %coord_ref.3) | copy-start | bytes 73732
  81.0 24.0 %all-to-all-start.3 = ((f32[64,2,128]{2,1,0:T(2,128)}), f32[64,2,128]{2,1,0:T(2,128)S(1)}, u32[]{:S(2)}, u32[]{:S(2)}) async-start(f32[64,2,128]{2,1,0:T(2,128)} %get-tuple-element.77), calls=%async_computation.3 | async-start | bytes 131072 | tf_op jit(solution)/shard_map/all_to_all | solution.py:437
  87.8 9.2 %collective-permute-start.7 = (f32[16,256]{1,0:T(8,128)S(1)}, f32[16,256]{1,0:T(8,128)S(1)}, u32[]{:S(2)}, u32[]{:S(2)}) collective-permute-start(f32[16,256]{1,0:T(8,128)S(1)} %get-tuple-element.71), channel_id=1, source_target_pairs={{0,64},{64,128},{128,192},{192,0},{1,65},{65,129},{129,193},{193,1... | collective-permute-start | bytes 49160 | tf_op jit(solution)/shard_map/ppermute | solution.py:444
  88.4 8.5 %collective-permute-start.8 = (f32[16,256]{1,0:T(8,128)S(1)}, f32[16,256]{1,0:T(8,128)S(1)}, u32[]{:S(2)}, u32[]{:S(2)}) collective-permute-start(f32[16,256]{1,0:T(8,128)S(1)} %get-tuple-element.72), channel_id=1, source_target_pairs={{64,0},{128,64},{192,128},{0,192},{65,1},{129,65},{193,129},{1,193... | collective-permute-start | bytes 49160 | tf_op jit(solution)/shard_map/ppermute | solution.py:445
  91.3 5.7 %collective-permute-start.9 = (f32[16,256]{1,0:T(8,128)S(1)}, f32[16,256]{1,0:T(8,128)S(1)}, u32[]{:S(2)}, u32[]{:S(2)}) collective-permute-start(f32[16,256]{1,0:T(8,128)S(1)} %get-tuple-element.73), channel_id=1, source_target_pairs={{0,8},{8,16},{16,24},{24,32},{32,40},{40,48},{48,56},{56,0},{1,9},... | collective-permute-start | bytes 49160 | tf_op jit(solution)/shard_map/ppermute | solution.py:444
  91.3 5.7 %collective-permute-start.10 = (f32[16,256]{1,0:T(8,128)S(1)}, f32[16,256]{1,0:T(8,128)S(1)}, u32[]{:S(2)}, u32[]{:S(2)}) collective-permute-start(f32[16,256]{1,0:T(8,128)S(1)} %get-tuple-element.74), channel_id=1, source_target_pairs={{8,0},{16,8},{24,16},{32,24},{40,32},{48,40},{56,48},{0,56},{9,1},... | collective-permute-start | bytes 49160 | tf_op jit(solution)/shard_map/ppermute | solution.py:445
  94.3 4.1 %collective-permute-start.11 = (f32[16,256]{1,0:T(8,128)S(1)}, f32[16,256]{1,0:T(8,128)S(1)}, u32[]{:S(2)}, u32[]{:S(2)}) collective-permute-start(f32[16,256]{1,0:T(8,128)S(1)} %get-tuple-element.75), channel_id=1, source_target_pairs={{0,1},{1,2},{2,3},{3,4},{4,5},{5,6},{6,7},{7,0},{8,9},{9,10},{10,1... | collective-permute-start | bytes 49160 | tf_op jit(solution)/shard_map/ppermute | solution.py:444
  97.0 5.0 %collective-permute-start.12 = (f32[16,256]{1,0:T(8,128)S(1)}, f32[16,256]{1,0:T(8,128)S(1)}, u32[]{:S(2)}, u32[]{:S(2)}) collective-permute-start(f32[16,256]{1,0:T(8,128)S(1)} %get-tuple-element.76), channel_id=1, source_target_pairs={{1,0},{2,1},{3,2},{4,3},{5,4},{6,5},{7,6},{0,7},{9,8},{10,9},{11,1... | collective-permute-start | bytes 49160 | tf_op jit(solution)/shard_map/ppermute | solution.py:445
where the time goes:
time: 107 us; the launch traced here: 106 us
  starting transfers between devices  42.9 us (40%)
  Pallas kernels  28.4 us (27%)
  waiting for transfers between devices  16.5 us (15%)
  blocking collectives  15.7 us (15%)
  between operations  1.42 us (1%)
    pallas_call x9, Pallas kernels, run(): pl.pallas_call(kernel, out_shape=shapes, in_specs=[smem] * scalars + [vme...  28.4 us
    all_to_all x3, starting transfers between devices, exchange(): lax.all_to_all(block, ('gy', 'gz'), split_axis=0, concat_axis=0, tiled=True)  24.2 us
    all_to_all x1, blocking collectives, exchange(): lax.all_to_all(block, ('gy', 'gz'), split_axis=0, concat_axis=0, tiled=True)  15.7 us
    ppermute x6, starting transfers between devices, neighbour_faces(): lax.ppermute(sends[2 * axis_index], axis, [(b, a) for a, b in up])  10.5 us
    ppermute x6, starting transfers between devices, neighbour_faces(): arrived[2 * axis_index] = lax.ppermute(sends[2 * axis_index + 1], axis, up)  7.59 us
    ppermute x6, waiting for transfers between devices, neighbour_faces(): lax.ppermute(sends[2 * axis_index], axis, [(b, a) for a, b in up])  7.03 us
    ppermute x1, waiting for transfers between devices, local(): lax.ppermute(code_rate, ('gy', 'gz'), [((i + 1) % owners, i) for i in ran...  5.34 us
    all_to_all x3, waiting for transfers between devices, exchange(): lax.all_to_all(block, ('gy', 'gz'), split_axis=0, concat_axis=0, tiled=True)  2.17 us
  transfers between devices with their start and end apart: 16, of which 6 were waited for; matrix products, arithmetic and copies ran while one was open for 0% of the time, Pallas kernels for 9%

commit v1 on v0

--- a/solution.py
+++ b/solution.py
@@ -30,18 +30,27 @@
 i32 = jnp.int32
 
 
-def laplace_table():
+def second_table():
     differences = node_points[:, None] - node_points[None, :] + np.eye(8)
     weights = 1.0 / np.prod(differences, axis=1)
     derivative = weights[None, :] / weights[:, None] / differences
     derivative = derivative * (1.0 - np.eye(8))
     derivative = derivative - np.eye(8) * derivative.sum(axis=1)[:, None]
     second = derivative @ derivative
-    identity = np.eye(8)
-    operator = np.kron(np.kron(second, identity), identity)
-    operator = operator + np.kron(np.kron(identity, second), identity)
-    operator = operator + np.kron(np.kron(identity, identity), second)
-    return operator.T
+    return second
+
+
+def laplace_tables():
+    second = second_table()
+    plane = np.kron(second, np.eye(8)) + np.kron(np.eye(8), second)
+    factors = np.zeros((32, 128))
+    for s in range(4):
+        for t in range(4):
+            factors[8 * s + 2 * t, :64] = second[2 * s, 2 * t]
+            factors[8 * s + 2 * t, 64:] = second[2 * s + 1, 2 * t + 1]
+            factors[8 * s + 2 * t + 1, :64] = second[2 * s, 2 * t + 1]
+            factors[8 * s + 2 * t + 1, 64:] = second[2 * s + 1, 2 * t]
+    return np.kron(np.eye(2), plane).T, factors
 
 
 def face_table():
@@ -354,7 +363,7 @@
     code_ref[...] = owner * CAP + rank_in_owner(owner).astype(i32)
 
 
-def fluid_kernel(again, state_ref, force_ref, own_ref, far_ref, lap_high_ref, lap_low_ref, keep_ref, faces_ref, *refs):
+def fluid_kernel(again, state_ref, force_ref, own_ref, far_ref, plane_ref, factor_ref, keep_ref, faces_ref, *refs):
     halo_refs, refs = refs[:6], refs[6:]
     if again:
         chosen_ref, out_ref, next_ref = refs[:3]
@@ -385,9 +394,19 @@
     spread = dot_nt(jnp.concatenate([high, low], axis=0), select)
     spread = spread[: 4 * ELEMS] + spread[4 * ELEMS :]
     state = state_ref[...].reshape(4 * ELEMS, 512)
-    high, low = split(state)
-    wide = dot(jnp.concatenate([high, low], axis=0), lap_high_ref[...])
-    laplace = wide[: 4 * ELEMS] + wide[4 * ELEMS :] + dot(high, lap_low_ref[...])
+    tiles = [state[:, t * 128 : (t + 1) * 128] for t in range(4)]
+    swapped = [pltpu.roll(tile, 64, 1) for tile in tiles]
+    laplace = []
+    for s in range(4):
+        high, low = split(tiles[s])
+        wide = dot(jnp.concatenate([high, low], axis=0), plane_ref[0:128])
+        part = wide[: 4 * ELEMS] + wide[4 * ELEMS :] + dot(high, plane_ref[128:256])
+        for t in range(4):
+            row = 8 * s + 2 * t
+            part = part + factor_ref[row : row + 1, :] * tiles[t]
+            part = part + factor_ref[row + 1 : row + 2, :] * swapped[t]
+        laplace.append(part)
+    laplace = jnp.concatenate(laplace, axis=1)
     result = state * keep_ref[...] + viscosity * laplace + penalty * spread
     row = iota((4 * ELEMS, 1), 0)
     result = result + jnp.where(row < 3 * ELEMS, -loading, heating) * force_ref[...]
@@ -426,9 +445,11 @@
 def local(field, neighbours, cell_one, ref_one, cell_two, ref_two, velocity, rate, cut):
     device = lax.axis_index(("gx", "gy", "gz")).astype(i32).reshape(1)
     near_t = neighbours.T
-    lap = laplace_table()
-    lap_high = jnp.asarray(lap, bf16)
-    lap_low = jnp.asarray(lap - np.asarray(np.asarray(lap, bf16), np.float64), bf16)
+    plane, factors = laplace_tables()
+    plane_high = np.asarray(plane, bf16)
+    plane_low = np.asarray(plane - np.asarray(plane_high, np.float64), bf16)
+    plane = jnp.asarray(np.concatenate([plane_high, plane_low], axis=0))
+    factors = jnp.asarray(factors, f32)
     keep = jnp.asarray(1.0 - penalty * face_table().sum(axis=1), f32)[None]
     row_one, row_two = cell_one[None], cell_two[None]
     slots = close(OWNERS, 4, 128)
@@ -491,7 +512,7 @@
     code_two, own, far = call(
         tables_kernel, [close(1, BIN, dtype=i32)] + hots, scalars=1, near=(1, 2)
     )(device, near_t, row_two)
-    tables = (own, far, lap_high, lap_low, keep)
+    tables = (own, far, plane, factors, keep)
     middle, faces, *sends = call(
         functools.partial(fluid_kernel, True), [close(4, ELEMS, 512)] + face_shapes, near=(1, 2, 3, 7, 8, 9, 10, 11, 12, 13)
     )(field, force, *tables, faces, *arrived, chosen)

time: 107 us -> 106 us (level)
  transfers between devices with their start and end apart: 16 -> 16, of which waited for: 6 -> 6; matrix products, arithmetic and copies ran while one was open for 0% -> 0% of each run, Pallas kernels for 9% -> 8%
where the time goes in v1:
time: 106 us
  starting transfers between devices  42.9 us (40%)
  Pallas kernels  27.9 us (26%)
  waiting for transfers between devices  16.5 us (16%)
  blocking collectives  15.7 us (15%)
  between operations  1.42 us (1%)
  local copies, waits for them, and re-layouts  1.06 us (1%)
    pallas_call x9, Pallas kernels, run(): pl.pallas_call(kernel, out_shape=shapes, in_specs=[smem] * scalars + [vme...  27.9 us
    all_to_all x3, starting transfers between devices, exchange(): lax.all_to_all(block, ('gy', 'gz'), split_axis=0, concat_axis=0, tiled=True)  24.2 us
    all_to_all x1, blocking collectives, exchange(): lax.all_to_all(block, ('gy', 'gz'), split_axis=0, concat_axis=0, tiled=True)  15.7 us
    ppermute x6, starting transfers between devices, neighbour_faces(): lax.ppermute(sends[2 * axis_index], axis, [(b, a) for a, b in up])  10.4 us
    ppermute x6, starting transfers between devices, neighbour_faces(): arrived[2 * axis_index] = lax.ppermute(sends[2 * axis_index + 1], axis, up)  7.6 us
    ppermute x6, waiting for transfers between devices, neighbour_faces(): lax.ppermute(sends[2 * axis_index], axis, [(b, a) for a, b in up])  7.03 us
    ppermute x1, waiting for transfers between devices, local(): lax.ppermute(code_rate, ('gy', 'gz'), [((i + 1) % owners, i) for i in ran...  5.34 us
    all_to_all x3, waiting for transfers between devices, exchange(): lax.all_to_all(block, ('gy', 'gz'), split_axis=0, concat_axis=0, tiled=True)  2.17 us
  transfers between devices with their start and end apart: 16, of which 6 were waited for; matrix products, arithmetic and copies ran while one was open for 0% of the time, Pallas kernels for 8%

profile of v1, /device:TPU:96, one launch (start us, length us, event | category | flops | bytes accessed | tf_op | source)
XLA Modules:
  0.0 105.5 jit_solution(7955571839123503255)
XLA Ops:
  0.6 3.3 %shard_map.131 = (f32[64,4,128]{2,1,0:T(4,128)}, f32[2,2048]{1,0:T(2,128)}) custom-call(s32[1,2048]{1,0:T(1,128)} %bitcast.13, f32[3,2048]{1,0:T(4,128)} %coord_ref.2, f32[3,2048]{1,0:T(4,128)} %speed_ref.1, f32[1,2048]{1,0:T(1,128)} %bitcast.14), custom_call_target="tpu_custom_call" | custom-call | tf_op jit(solution)/shard_map/pallas_call | solution.py:426
  3.9 10.8 %all-to-all-start = ((f32[64,4,128]{2,1,0:T(4,128)}), f32[64,4,128]{2,1,0:T(4,128)S(1)}, u32[]{:S(2)}, u32[]{:S(2)}) async-start(f32[64,4,128]{2,1,0:T(4,128)} %get-tuple-element.40), calls=%async_computation | async-start | bytes 262144 | tf_op jit(solution)/shard_map/all_to_all | solution.py:458
  14.7 0.0 copy-done.4
  14.7 0.6 collective-permute-start
  16.0 5.3 %collective-permute-done = f32[2,2048]{1,0:T(2,128)S(1)} collective-permute-done((f32[2,2048]{1,0:T(2,128)S(1)}, f32[2,2048]{1,0:T(2,128)S(1)}, u32[]{:S(2)}, u32[]{:S(2)}) %collective-permute-start) | collective-permute-done | bytes 16416 | tf_op jit(solution)/shard_map/ppermute | solution.py:496
  21.4 0.1 fusion.moved_ref
  21.5 2.2 %all-to-all-done.incoming_ref = f32[64,4,128]{2,1,0:T(4,128)S(1)} async-done(((f32[64,4,128]{2,1,0:T(4,128)}), f32[64,4,128]{2,1,0:T(4,128)S(1)}, u32[]{:S(2)}, u32[]{:S(2)}) %all-to-all-start) | async-done | bytes 131104 | tf_op jit(solution)/shard_map/all_to_all | solution.py:458
  23.7 1.0 copy-done
  24.7 6.5 %shard_map.132 = (f32[64,4,128]{2,1,0:T(4,128)}, f32[256,512]{1,0:T(8,128)S(1)}) custom-call(f32[64,4,128]{2,1,0:T(4,128)S(1)} %all-to-all-done.incoming_ref, f32[4,64,512]{2,1,0:T(8,128)S(1)} %copy-done), custom_call_target="tpu_custom_call" | custom-call | tf_op jit(solution)/shard_map/pallas_call | solution.py:426
  31.2 6.6 %all-to-all-start.1 = ((f32[64,4,128]{2,1,0:T(4,128)}), f32[64,4,128]{2,1,0:T(4,128)S(1)}, u32[]{:S(2)}, u32[]{:S(2)}) async-start(f32[64,4,128]{2,1,0:T(4,128)} %get-tuple-element.43), calls=%async_computation.1 | async-start | bytes 262144 | tf_op jit(solution)/shard_map/all_to_all | solution.py:458
  37.9 2.2 %shard_map.134 = (bf16[6,16,64]{2,1,0:T(8,128)(2,1)}, f32[6,64,256]{2,1,0:T(8,128)S(1)}, f32[16,256]{1,0:T(8,128)S(1)}, f32[16,256]{1,0:T(8,128)S(1)}, f32[16,25...) custom-call(s32[1]{0:T(128)} %bitcast.5.device_ref, ...), custom_call_target="tpu_custom_call" | custom-call | tf_op jit(solution)/shard_map/pallas_call | solution.py:426
  40.1 1.6 %collective-permute-start.1 = (f32[16,256]{1,0:T(8,128)S(1)}, f32[16,256]{1,0:T(8,128)S(1)}, u32[]{:S(2)}, u32[]{:S(2)}) collective-permute-start(f32[16,256]{1,0:T(8,128)S(1)} %get-tuple-element.51), channel_id=1, source_target_pairs={{0,64},{64,128},{128,192},{192,0},{1,65},{65,129},{129,193},{193,1... | collective-permute-start | bytes 49160 | tf_op jit(solution)/shard_map/ppermute | solution.py:465
  41.7 1.7 %collective-permute-start.2 = (f32[16,256]{1,0:T(8,128)S(1)}, f32[16,256]{1,0:T(8,128)S(1)}, u32[]{:S(2)}, u32[]{:S(2)}) collective-permute-start(f32[16,256]{1,0:T(8,128)S(1)} %get-tuple-element.52), channel_id=1, source_target_pairs={{64,0},{128,64},{192,128},{0,192},{65,1},{129,65},{193,129},{1,193... | collective-permute-start | bytes 49160 | tf_op jit(solution)/shard_map/ppermute | solution.py:466
  43.3 0.0 collective-permute-start.3
  43.3 3.0 %collective-permute-start.4 = (f32[16,256]{1,0:T(8,128)S(1)}, f32[16,256]{1,0:T(8,128)S(1)}, u32[]{:S(2)}, u32[]{:S(2)}) collective-permute-start(f32[16,256]{1,0:T(8,128)S(1)} %get-tuple-element.54), channel_id=1, source_target_pairs={{8,0},{16,8},{24,16},{32,24},{40,32},{48,40},{56,48},{0,56},{9,1},... | collective-permute-start | bytes 49160 | tf_op jit(solution)/shard_map/ppermute | solution.py:466
  46.3 2.7 %collective-permute-start.5 = (f32[16,256]{1,0:T(8,128)S(1)}, f32[16,256]{1,0:T(8,128)S(1)}, u32[]{:S(2)}, u32[]{:S(2)}) collective-permute-start(f32[16,256]{1,0:T(8,128)S(1)} %get-tuple-element.55), channel_id=1, source_target_pairs={{0,1},{1,2},{2,3},{3,4},{4,5},{5,6},{6,7},{7,0},{8,9},{9,10},{10,1... | collective-permute-start | bytes 49160 | tf_op jit(solution)/shard_map/ppermute | solution.py:465
  49.0 0.0 collective-permute-done.1.refs_0_
  49.0 0.0 collective-permute-start.6
  49.0 0.0 copy-done.2
  49.0 0.0 copy-done.3
  49.0 0.8 shard_map.133
  49.8 0.0 collective-permute-done.2.refs_1_
  49.8 0.0 collective-permute-done.3.refs_2_
  49.8 0.0 collective-permute-done.4.refs_3_
  49.9 0.6 collective-permute-done.5.refs_4_
  50.4 3.5 %collective-permute-done.6.refs_5_ = f32[16,256]{1,0:T(8,128)S(1)} collective-permute-done((f32[16,256]{1,0:T(8,128)S(1)}, f32[16,256]{1,0:T(8,128)S(1)}, u32[]{:S(2)}, u32[]{:S(2)}) %collective-permute-start.6) | collective-permute-done | bytes 16416 | tf_op jit(solution)/shard_map/ppermute | solution.py:466
  53.9 2.8 %shard_map.135 = (f32[4,64,512]{2,1,0:T(8,128)S(1)}, f32[6,64,256]{2,1,0:T(8,128)S(1)}, f32[16,256]{1,0:T(8,128)S(1)}, f32[16,256]{1,0:T(8,128)S(1)}, f32[16,256...) custom-call(f32[4,64,512]{2,1,0:T(8,128)} %state_ref.5, ...), custom_call_target="tpu_custom_call" | custom-call | tf_op jit(solution)/shard_map/pallas_call | solution.py:426
  56.8 0.0 all-to-all-done.1.back_ref
  56.8 0.0 copy-done.1
  56.8 1.8 %shard_map.136 = f32[64,4,128]{2,1,0:T(4,128)S(1)} custom-call(s32[1]{0:T(128)} %copy.14.cut_ref, f32[64,4,128]{2,1,0:T(4,128)S(1)} %all-to-all-done.1.back_ref, f32[2,2048]{1,0:T(2,128)S(1)} %fusion.moved_ref, s32[1,2048]{1,0:T(1,128)S(1)} %bitcast.10, s32[1,2048]{1,0:T(1,128)S(1)} %get-tuple-element.68.code_ref, f32[3,2048]{1,0:T(4,128)S(1)} %copy-done.1), custom_call_target="tpu_custom_call" | custom-call | tf_op jit(solution)/shard_map/pallas_call | solution.py:426
  58.6 15.7 %all_to_all.20.incoming_ref = f32[64,4,128]{2,1,0:T(4,128)S(1)} all-to-all(f32[64,4,128]{2,1,0:T(4,128)S(1)} %shard_map.136), channel_id=1, replica_groups=mesh['gx'=4,'gy'=8,'gz'=8] {'gy','gz'}, dimensions={0} | all-to-all | bytes 262144 | tf_op jit(solution)/shard_map/all_to_all | solution.py:458
  74.3 6.5 %shard_map.137 = (f32[64,2,128]{2,1,0:T(2,128)}, f32[256,512]{1,0:T(8,128)S(1)}) custom-call(f32[64,4,128]{2,1,0:T(4,128)S(1)} %all_to_all.20.incoming_ref, f32[4,64,512]{2,1,0:T(8,128)S(1)} %get-tuple-element.65.state_ref), custom_call_target="tpu_custom_call" | custom-call | tf_op jit(solution)/shard_map/pallas_call | solution.py:426
  80.8 6.7 %all-to-all-start.3 = ((f32[64,2,128]{2,1,0:T(2,128)}), f32[64,2,128]{2,1,0:T(2,128)S(1)}, u32[]{:S(2)}, u32[]{:S(2)}) async-start(f32[64,2,128]{2,1,0:T(2,128)} %get-tuple-element.77), calls=%async_computation.3 | async-start | bytes 131072 | tf_op jit(solution)/shard_map/all_to_all | solution.py:458
  87.5 0.7 collective-permute-start.7
  88.2 2.9 %collective-permute-start.8 = (f32[16,256]{1,0:T(8,128)S(1)}, f32[16,256]{1,0:T(8,128)S(1)}, u32[]{:S(2)}, u32[]{:S(2)}) collective-permute-start(f32[16,256]{1,0:T(8,128)S(1)} %get-tuple-element.72), channel_id=1, source_target_pairs={{64,0},{128,64},{192,128},{0,192},{65,1},{129,65},{193,129},{1,193... | collective-permute-start | bytes 49160 | tf_op jit(solution)/shard_map/ppermute | solution.py:466
  91.0 0.0 collective-permute-start.9
  91.0 3.0 %collective-permute-start.10 = (f32[16,256]{1,0:T(8,128)S(1)}, f32[16,256]{1,0:T(8,128)S(1)}, u32[]{:S(2)}, u32[]{:S(2)}) collective-permute-start(f32[16,256]{1,0:T(8,128)S(1)} %get-tuple-element.74), channel_id=1, source_target_pairs={{8,0},{16,8},{24,16},{32,24},{40,32},{48,40},{56,48},{0,56},{9,1},... | collective-permute-start | bytes 49160 | tf_op jit(solution)/shard_map/ppermute | solution.py:466
  94.0 2.7 %collective-permute-start.11 = (f32[16,256]{1,0:T(8,128)S(1)}, f32[16,256]{1,0:T(8,128)S(1)}, u32[]{:S(2)}, u32[]{:S(2)}) collective-permute-start(f32[16,256]{1,0:T(8,128)S(1)} %get-tuple-element.75), channel_id=1, source_target_pairs={{0,1},{1,2},{2,3},{3,4},{4,5},{5,6},{6,7},{7,0},{8,9},{9,10},{10,1... | collective-permute-start | bytes 49160 | tf_op jit(solution)/shard_map/ppermute | solution.py:465
  96.7 0.0 collective-permute-done.7.refs_0_
  96.7 0.0 collective-permute-start.12
  96.7 0.0 collective-permute-done.8.refs_1_
  96.7 0.0 collective-permute-done.9.refs_2_
  96.7 0.0 collective-permute-done.10.refs_3_
  96.7 1.4 %collective-permute-done.11.refs_4_ = f32[16,256]{1,0:T(8,128)S(1)} collective-permute-done((f32[16,256]{1,0:T(8,128)S(1)}, f32[16,256]{1,0:T(8,128)S(1)}, u32[]{:S(2)}, u32[]{:S(2)}) %collective-permute-start.11) | collective-permute-done | bytes 16416 | tf_op jit(solution)/shard_map/ppermute | solution.py:465
  98.1 3.5 %collective-permute-done.12.refs_5_ = f32[16,256]{1,0:T(8,128)S(1)} collective-permute-done((f32[16,256]{1,0:T(8,128)S(1)}, f32[16,256]{1,0:T(8,128)S(1)}, u32[]{:S(2)}, u32[]{:S(2)}) %collective-permute-start.12) | collective-permute-done | bytes 16416 | tf_op jit(solution)/shard_map/ppermute | solution.py:466
  101.6 2.8 %shard_map.138 = f32[4,64,512]{2,1,0:T(8,128)} custom-call(f32[4,64,512]{2,1,0:T(8,128)S(1)} %get-tuple-element.65.state_ref, f32[256,512]{1,0:T(8,128)S(1)} %get-tuple-element.69.force_ref, bf16[6,64,128]{2,1,0:T(8,128)(2,1)S(1)} %get-tuple-element.48.own_ref, bf16[6,64,32]{2,1,0:T(8,128)(2,1)S(1)} %get-tuple-element.49.far_ref, ...), custom_call_target="tpu_custom_call" | custom-call | tf_op jit(solution)/shard_map/pallas_call | solution.py:426
  104.5 0.0 all-to-all-done.3.back_ref
  104.5 1.1 %shard_map.139 = f32[3,2048]{1,0:T(4,128)} custom-call(f32[64,2,128]{2,1,0:T(2,128)S(1)} %all-to-all-done.3.back_ref, s32[1,2048]{1,0:T(1,128)S(1)} %get-tuple-element.68.code_ref), custom_call_target="tpu_custom_call" | custom-call | tf_op jit(solution)/shard_map/pallas_call | solution.py:426
  (5 shorter events, 0.0 us)
Async XLA Ops:
  3.9 10.8 %copy-start.4 = (f32[2,2048]{1,0:T(2,128)S(1)}, f32[2,2048]{1,0:T(2,128)}, u32[]{:S(2)}) copy-start(f32[2,2048]{1,0:T(2,128)} %get-tuple-element.41) | copy-start | bytes 49156
  3.9 19.8 %all-to-all-start = ((f32[64,4,128]{2,1,0:T(4,128)}), f32[64,4,128]{2,1,0:T(4,128)S(1)}, u32[]{:S(2)}, u32[]{:S(2)}) async-start(f32[64,4,128]{2,1,0:T(4,128)} %get-tuple-element.40), calls=%async_computation | async-start | bytes 262144 | tf_op jit(solution)/shard_map/all_to_all | solution.py:458
  14.7 6.6 %collective-permute-start = (f32[2,2048]{1,0:T(2,128)S(1)}, f32[2,2048]{1,0:T(2,128)S(1)}, u32[]{:S(2)}, u32[]{:S(2)}) collective-permute-start(f32[2,2048]{1,0:T(2,128)S(1)} %copy-done.4), channel_id=1, source_target_pairs={{1,0},{2,1},{3,2},{4,3},{5,4},{6,5},{7,6},{8,7},{9,8},{10,9},{11,1... | collective-permute-start | bytes 49160 | tf_op jit(solution)/shard_map/ppermute | solution.py:496
  23.7 1.0 copy-start
  31.2 25.5 %all-to-all-start.1 = ((f32[64,4,128]{2,1,0:T(4,128)}), f32[64,4,128]{2,1,0:T(4,128)S(1)}, u32[]{:S(2)}, u32[]{:S(2)}) async-start(f32[64,4,128]{2,1,0:T(4,128)} %get-tuple-element.43), calls=%async_computation.1 | async-start | bytes 262144 | tf_op jit(solution)/shard_map/all_to_all | solution.py:458
  40.1 8.9 %copy-start.2 = (s32[2048]{0:T(1024)S(1)}, s32[2048]{0:T(1024)}, u32[]{:S(2)}) copy-start(s32[2048]{0:T(1024)} %param.16) | copy-start | bytes 24580
  40.1 8.9 %collective-permute-start.1 = (f32[16,256]{1,0:T(8,128)S(1)}, f32[16,256]{1,0:T(8,128)S(1)}, u32[]{:S(2)}, u32[]{:S(2)}) collective-permute-start(f32[16,256]{1,0:T(8,128)S(1)} %get-tuple-element.51), channel_id=1, source_target_pairs={{0,64},{64,128},{128,192},{192,0},{1,65},{65,129},{129,193},{193,1... | collective-permute-start | bytes 49160 | tf_op jit(solution)/shard_map/ppermute | solution.py:465
  41.7 8.2 %collective-permute-start.2 = (f32[16,256]{1,0:T(8,128)S(1)}, f32[16,256]{1,0:T(8,128)S(1)}, u32[]{:S(2)}, u32[]{:S(2)}) collective-permute-start(f32[16,256]{1,0:T(8,128)S(1)} %get-tuple-element.52), channel_id=1, source_target_pairs={{64,0},{128,64},{192,128},{0,192},{65,1},{129,65},{193,129},{1,193... | collective-permute-start | bytes 49160 | tf_op jit(solution)/shard_map/ppermute | solution.py:466
  43.3 6.5 %collective-permute-start.3 = (f32[16,256]{1,0:T(8,128)S(1)}, f32[16,256]{1,0:T(8,128)S(1)}, u32[]{:S(2)}, u32[]{:S(2)}) collective-permute-start(f32[16,256]{1,0:T(8,128)S(1)} %get-tuple-element.53), channel_id=1, source_target_pairs={{0,8},{8,16},{16,24},{24,32},{32,40},{40,48},{48,56},{56,0},{1,9},... | collective-permute-start | bytes 49160 | tf_op jit(solution)/shard_map/ppermute | solution.py:465
  43.3 5.7 %copy-start.3 = (s32[64,6]{0,1:T(8,128)S(1)}, s32[64,6]{0,1:T(8,128)}, u32[]{:S(2)}) copy-start(s32[64,6]{0,1:T(8,128)} %param.13) | copy-start | bytes 4612
  43.3 6.5 %collective-permute-start.4 = (f32[16,256]{1,0:T(8,128)S(1)}, f32[16,256]{1,0:T(8,128)S(1)}, u32[]{:S(2)}, u32[]{:S(2)}) collective-permute-start(f32[16,256]{1,0:T(8,128)S(1)} %get-tuple-element.54), channel_id=1, source_target_pairs={{8,0},{16,8},{24,16},{32,24},{40,32},{48,40},{56,48},{0,56},{9,1},... | collective-permute-start | bytes 49160 | tf_op jit(solution)/shard_map/ppermute | solution.py:466
  46.3 4.1 %collective-permute-start.5 = (f32[16,256]{1,0:T(8,128)S(1)}, f32[16,256]{1,0:T(8,128)S(1)}, u32[]{:S(2)}, u32[]{:S(2)}) collective-permute-start(f32[16,256]{1,0:T(8,128)S(1)} %get-tuple-element.55), channel_id=1, source_target_pairs={{0,1},{1,2},{2,3},{3,4},{4,5},{5,6},{6,7},{7,0},{8,9},{9,10},{10,1... | collective-permute-start | bytes 49160 | tf_op jit(solution)/shard_map/ppermute | solution.py:465
  49.0 5.0 %collective-permute-start.6 = (f32[16,256]{1,0:T(8,128)S(1)}, f32[16,256]{1,0:T(8,128)S(1)}, u32[]{:S(2)}, u32[]{:S(2)}) collective-permute-start(f32[16,256]{1,0:T(8,128)S(1)} %get-tuple-element.56), channel_id=1, source_target_pairs={{1,0},{2,1},{3,2},{4,3},{5,4},{6,5},{7,6},{0,7},{9,8},{10,9},{11,1... | collective-permute-start | bytes 49160 | tf_op jit(solution)/shard_map/ppermute | solution.py:466
  53.9 2.9 %copy-start.1 = (f32[3,2048]{1,0:T(4,128)S(1)}, f32[3,2048]{1,0:T(4,128)}, u32[]{:S(2)}) copy-start(f32[3,2048]{1,0:T(4,128)} %coord_ref.3) | copy-start | bytes 73732
  80.8 23.7 %all-to-all-start.3 = ((f32[64,2,128]{2,1,0:T(2,128)}), f32[64,2,128]{2,1,0:T(2,128)S(1)}, u32[]{:S(2)}, u32[]{:S(2)}) async-start(f32[64,2,128]{2,1,0:T(2,128)} %get-tuple-element.77), calls=%async_computation.3 | async-start | bytes 131072 | tf_op jit(solution)/shard_map/all_to_all | solution.py:458
  87.5 9.2 %collective-permute-start.7 = (f32[16,256]{1,0:T(8,128)S(1)}, f32[16,256]{1,0:T(8,128)S(1)}, u32[]{:S(2)}, u32[]{:S(2)}) collective-permute-start(f32[16,256]{1,0:T(8,128)S(1)} %get-tuple-element.71), channel_id=1, source_target_pairs={{0,64},{64,128},{128,192},{192,0},{1,65},{65,129},{129,193},{193,1... | collective-permute-start | bytes 49160 | tf_op jit(solution)/shard_map/ppermute | solution.py:465
  88.2 8.5 %collective-permute-start.8 = (f32[16,256]{1,0:T(8,128)S(1)}, f32[16,256]{1,0:T(8,128)S(1)}, u32[]{:S(2)}, u32[]{:S(2)}) collective-permute-start(f32[16,256]{1,0:T(8,128)S(1)} %get-tuple-element.72), channel_id=1, source_target_pairs={{64,0},{128,64},{192,128},{0,192},{65,1},{129,65},{193,129},{1,193... | collective-permute-start | bytes 49160 | tf_op jit(solution)/shard_map/ppermute | solution.py:466
  91.0 5.7 %collective-permute-start.9 = (f32[16,256]{1,0:T(8,128)S(1)}, f32[16,256]{1,0:T(8,128)S(1)}, u32[]{:S(2)}, u32[]{:S(2)}) collective-permute-start(f32[16,256]{1,0:T(8,128)S(1)} %get-tuple-element.73), channel_id=1, source_target_pairs={{0,8},{8,16},{16,24},{24,32},{32,40},{40,48},{48,56},{56,0},{1,9},... | collective-permute-start | bytes 49160 | tf_op jit(solution)/shard_map/ppermute | solution.py:465
  91.0 5.7 %collective-permute-start.10 = (f32[16,256]{1,0:T(8,128)S(1)}, f32[16,256]{1,0:T(8,128)S(1)}, u32[]{:S(2)}, u32[]{:S(2)}) collective-permute-start(f32[16,256]{1,0:T(8,128)S(1)} %get-tuple-element.74), channel_id=1, source_target_pairs={{8,0},{16,8},{24,16},{32,24},{40,32},{48,40},{56,48},{0,56},{9,1},... | collective-permute-start | bytes 49160 | tf_op jit(solution)/shard_map/ppermute | solution.py:466
  94.0 4.1 %collective-permute-start.11 = (f32[16,256]{1,0:T(8,128)S(1)}, f32[16,256]{1,0:T(8,128)S(1)}, u32[]{:S(2)}, u32[]{:S(2)}) collective-permute-start(f32[16,256]{1,0:T(8,128)S(1)} %get-tuple-element.75), channel_id=1, source_target_pairs={{0,1},{1,2},{2,3},{3,4},{4,5},{5,6},{6,7},{7,0},{8,9},{9,10},{10,1... | collective-permute-start | bytes 49160 | tf_op jit(solution)/shard_map/ppermute | solution.py:465
  96.7 5.0 %collective-permute-start.12 = (f32[16,256]{1,0:T(8,128)S(1)}, f32[16,256]{1,0:T(8,128)S(1)}, u32[]{:S(2)}, u32[]{:S(2)}) collective-permute-start(f32[16,256]{1,0:T(8,128)S(1)} %get-tuple-element.76), channel_id=1, source_target_pairs={{1,0},{2,1},{3,2},{4,3},{5,4},{6,5},{7,6},{0,7},{9,8},{10,9},{11,1... | collective-permute-start | bytes 49160 | tf_op jit(solution)/shard_map/ppermute | solution.py:466

commit v2 on v1

--- a/solution.py
+++ b/solution.py
@@ -172,25 +172,36 @@
     scatter_slots(out_ref, owner, rank.astype(i32), values)
 
 
-def resend_kernel(cut_ref, back_ref, moved_ref, cell_ref, code_ref, coord_ref, out_ref):
+def known_kernel(moved_ref, cell_ref, code_ref, coord_ref, out_ref):
+    code = code_ref[...]
+    element = (cell_ref[...] & (ELEMS - 1)).astype(f32)
+    zero = jnp.zeros((1, BIN), f32)
+    values = [element, zero, coord_ref[0:1, :], zero, coord_ref[1:2, :], zero, coord_ref[2:3, :], moved_ref[1:2, :]]
+    scatter_slots(out_ref, code >> 6, code & (CAP - 1), values)
+
+
+def resend_kernel(cut_ref, back_ref, moved_ref, known_ref, code_ref, out_ref):
     first_code = moved_ref[0:1, :].astype(i32)
-    rate = moved_ref[1:2, :]
     part = jnp.where(iota((1, BIN), 1) + cut_ref[0] >= BIN, CAP, 0)
     lane_hot = one_hot((first_code & (CAP - 1)) + part, 128)
     speeds = gather_slots([back_ref[:, k, :] for k in range(3)], first_code >> 6, lane_hot)
-    element = (cell_ref[...] & (ELEMS - 1)).astype(f32)
     code = code_ref[...]
-    values = [
-        element,
-        speeds[0],
-        coord_ref[0:1, :],
-        speeds[1],
-        coord_ref[1:2, :],
-        speeds[2],
-        coord_ref[2:3, :],
-        rate,
-    ]
-    scatter_slots(out_ref, code >> 6, code & (CAP - 1), values)
+    owned = one_hot(code >> 6, OWNERS)
+    placed = one_hot(code & (CAP - 1), CAP)
+    empty = jnp.zeros((CAP, BIN), bf16)
+    highs, lows = [], []
+    for k in range(3):
+        high, low = split_row(speeds[k])
+        highs.append(placed * thick(high, CAP))
+        lows.append(placed * thick(low, CAP))
+    out = dot_nt(owned, jnp.concatenate([highs[1], highs[0], empty, highs[2]], axis=0)) + dot_nt(
+        owned, jnp.concatenate([lows[1], lows[0], empty, lows[2]], axis=0)
+    )
+    left = iota((OWNERS, 128), 1) < 64
+    pair, last = out[:, :128], out[:, 128:]
+    for j, speed in enumerate((pair, pltpu.roll(pair, 64, 1), last)):
+        out_ref[:, j, :] = jnp.where(left, known_ref[:, j, :], speed)
+    out_ref[:, 3, :] = known_ref[:, 3, :]
 
 
 def final_kernel(back_ref, code_ref, out_ref):
@@ -512,15 +523,16 @@
     code_two, own, far = call(
         tables_kernel, [close(1, BIN, dtype=i32)] + hots, scalars=1, near=(1, 2)
     )(device, near_t, row_two)
+    known = call(known_kernel, slots, near=(0, 1, 2, 3))(
+        moved, row_two, code_two, ref_two
+    )
     tables = (own, far, plane, factors, keep)
     middle, faces, *sends = call(
         functools.partial(fluid_kernel, True), [close(4, ELEMS, 512)] + face_shapes, near=(1, 2, 3, 7, 8, 9, 10, 11, 12, 13)
     )(field, force, *tables, faces, *arrived, chosen)
-    returned, middle, *sends = lax.optimization_barrier((returned, middle, *sends))
+    returned, middle, known, *sends = lax.optimization_barrier((returned, middle, known, *sends))
     arrived = neighbour_faces(sends)
-    outgoing = call(resend_kernel, slots, scalars=1, near=(1, 2, 3, 4, 5))(
-        cut, returned, moved, row_two, code_two, ref_two
-    )
+    outgoing = call(resend_kernel, slots, scalars=1, near=(1, 2, 3, 4))(cut, returned, moved, known, code_two)
     incoming = exchange(outgoing)
     back, force = particles(incoming, middle, False)
     returned = exchange(back)

time: 106 us -> 106 us (level)
  waiting for transfers between devices: 16.5 us -> 15 us
    pallas_call x9 -> x10, Pallas kernels: 27.9 us -> 28.8 us  [run(): pl.pallas_call(kernel, out_shape=shapes, in_specs=[smem] * scalars + [vme...]
  transfers between devices with their start and end apart: 16 -> 16, of which waited for: 6 -> 5; matrix products, arithmetic and copies ran while one was open for 0% -> 0% of each run, Pallas kernels for 8% -> 10%
where the time goes in v2:
time: 106 us; the launch traced here: 105 us
  starting transfers between devices  42.9 us (40%)
  Pallas kernels  28.8 us (27%)
  blocking collectives  15.8 us (15%)
  waiting for transfers between devices  15 us (14%)
  between operations  1.45 us (1%)
  local copies, waits for them, and re-layouts  1.06 us (1%)
    pallas_call x10, Pallas kernels, run(): pl.pallas_call(kernel, out_shape=shapes, in_specs=[smem] * scalars + [vme...  28.8 us
    all_to_all x3, starting transfers between devices, exchange(): lax.all_to_all(block, ('gy', 'gz'), split_axis=0, concat_axis=0, tiled=True)  24.4 us
    all_to_all x1, blocking collectives, exchange(): lax.all_to_all(block, ('gy', 'gz'), split_axis=0, concat_axis=0, tiled=True)  15.8 us
    ppermute x6, starting transfers between devices, neighbour_faces(): lax.ppermute(sends[2 * axis_index], axis, [(b, a) for a, b in up])  10.5 us
    ppermute x6, starting transfers between devices, neighbour_faces(): arrived[2 * axis_index] = lax.ppermute(sends[2 * axis_index + 1], axis, up)  7.37 us
    ppermute x6, waiting for transfers between devices, neighbour_faces(): lax.ppermute(sends[2 * axis_index], axis, [(b, a) for a, b in up])  6.1 us
    ppermute x1, waiting for transfers between devices, local(): lax.ppermute(code_rate, ('gy', 'gz'), [((i + 1) % owners, i) for i in ran...  5.34 us
    all_to_all x3, waiting for transfers between devices, exchange(): lax.all_to_all(block, ('gy', 'gz'), split_axis=0, concat_axis=0, tiled=True)  2.17 us
  transfers between devices with their start and end apart: 16, of which 5 were waited for; matrix products, arithmetic and copies ran while one was open for 0% of the time, Pallas kernels for 10%

profile of v2, /device:TPU:96, one launch (start us, length us, event | category | flops | bytes accessed | tf_op | source)
XLA Modules:
  0.0 105.1 jit_solution(11983215832414358858)
XLA Ops:
  0.6 3.3 %shard_map.131 = (f32[64,4,128]{2,1,0:T(4,128)}, f32[2,2048]{1,0:T(2,128)}) custom-call(s32[1,2048]{1,0:T(1,128)} %bitcast.13, f32[3,2048]{1,0:T(4,128)} %coord_ref.2, f32[3,2048]{1,0:T(4,128)} %speed_ref.1, f32[1,2048]{1,0:T(1,128)} %bitcast.14), custom_call_target="tpu_custom_call" | custom-call | tf_op jit(solution)/shard_map/pallas_call | solution.py:437
  3.9 10.8 %all-to-all-start = ((f32[64,4,128]{2,1,0:T(4,128)}), f32[64,4,128]{2,1,0:T(4,128)S(1)}, u32[]{:S(2)}, u32[]{:S(2)}) async-start(f32[64,4,128]{2,1,0:T(4,128)} %get-tuple-element.41), calls=%async_computation | async-start | bytes 262144 | tf_op jit(solution)/shard_map/all_to_all | solution.py:469
  14.7 0.0 copy-done.4
  14.7 0.6 collective-permute-start
  16.0 5.3 %collective-permute-done = f32[2,2048]{1,0:T(2,128)S(1)} collective-permute-done((f32[2,2048]{1,0:T(2,128)S(1)}, f32[2,2048]{1,0:T(2,128)S(1)}, u32[]{:S(2)}, u32[]{:S(2)}) %collective-permute-start) | collective-permute-done | bytes 16416 | tf_op jit(solution)/shard_map/ppermute | solution.py:507
  21.4 0.1 fusion.moved_ref
  21.5 2.2 %all-to-all-done.incoming_ref = f32[64,4,128]{2,1,0:T(4,128)S(1)} async-done(((f32[64,4,128]{2,1,0:T(4,128)}), f32[64,4,128]{2,1,0:T(4,128)S(1)}, u32[]{:S(2)}, u32[]{:S(2)}) %all-to-all-start) | async-done | bytes 131104 | tf_op jit(solution)/shard_map/all_to_all | solution.py:469
  23.7 1.0 copy-done
  24.7 6.5 %shard_map.132 = (f32[64,4,128]{2,1,0:T(4,128)}, f32[256,512]{1,0:T(8,128)S(1)}) custom-call(f32[64,4,128]{2,1,0:T(4,128)S(1)} %all-to-all-done.incoming_ref, f32[4,64,512]{2,1,0:T(8,128)S(1)} %copy-done), custom_call_target="tpu_custom_call" | custom-call | tf_op jit(solution)/shard_map/pallas_call | solution.py:437
  31.2 6.6 %all-to-all-start.1 = ((f32[64,4,128]{2,1,0:T(4,128)}), f32[64,4,128]{2,1,0:T(4,128)S(1)}, u32[]{:S(2)}, u32[]{:S(2)}) async-start(f32[64,4,128]{2,1,0:T(4,128)} %get-tuple-element.44), calls=%async_computation.1 | async-start | bytes 262144 | tf_op jit(solution)/shard_map/all_to_all | solution.py:469
  37.9 0.0 copy-start.2
  37.9 2.2 %shard_map.134 = (bf16[6,16,64]{2,1,0:T(8,128)(2,1)}, f32[6,64,256]{2,1,0:T(8,128)S(1)}, f32[16,256]{1,0:T(8,128)S(1)}, f32[16,256]{1,0:T(8,128)S(1)}, f32[16,25...) custom-call(s32[1]{0:T(128)} %bitcast.5.device_ref, ...), custom_call_target="tpu_custom_call" | custom-call | tf_op jit(solution)/shard_map/pallas_call | solution.py:437
  40.1 1.6 %collective-permute-start.1 = (f32[16,256]{1,0:T(8,128)S(1)}, f32[16,256]{1,0:T(8,128)S(1)}, u32[]{:S(2)}, u32[]{:S(2)}) collective-permute-start(f32[16,256]{1,0:T(8,128)S(1)} %get-tuple-element.52), channel_id=1, source_target_pairs={{0,64},{64,128},{128,192},{192,0},{1,65},{65,129},{129,193},{193,1... | collective-permute-start | bytes 49160 | tf_op jit(solution)/shard_map/ppermute | solution.py:476
  41.7 1.7 %collective-permute-start.2 = (f32[16,256]{1,0:T(8,128)S(1)}, f32[16,256]{1,0:T(8,128)S(1)}, u32[]{:S(2)}, u32[]{:S(2)}) collective-permute-start(f32[16,256]{1,0:T(8,128)S(1)} %get-tuple-element.53), channel_id=1, source_target_pairs={{64,0},{128,64},{192,128},{0,192},{65,1},{129,65},{193,129},{1,193... | collective-permute-start | bytes 49160 | tf_op jit(solution)/shard_map/ppermute | solution.py:477
  43.3 0.0 collective-permute-start.3
  43.3 3.0 %collective-permute-start.4 = (f32[16,256]{1,0:T(8,128)S(1)}, f32[16,256]{1,0:T(8,128)S(1)}, u32[]{:S(2)}, u32[]{:S(2)}) collective-permute-start(f32[16,256]{1,0:T(8,128)S(1)} %get-tuple-element.55), channel_id=1, source_target_pairs={{8,0},{16,8},{24,16},{32,24},{40,32},{48,40},{56,48},{0,56},{9,1},... | collective-permute-start | bytes 49160 | tf_op jit(solution)/shard_map/ppermute | solution.py:477
  46.3 2.7 %collective-permute-start.5 = (f32[16,256]{1,0:T(8,128)S(1)}, f32[16,256]{1,0:T(8,128)S(1)}, u32[]{:S(2)}, u32[]{:S(2)}) collective-permute-start(f32[16,256]{1,0:T(8,128)S(1)} %get-tuple-element.56), channel_id=1, source_target_pairs={{0,1},{1,2},{2,3},{3,4},{4,5},{5,6},{6,7},{7,0},{8,9},{9,10},{10,1... | collective-permute-start | bytes 49160 | tf_op jit(solution)/shard_map/ppermute | solution.py:476
  49.0 0.0 collective-permute-done.1.refs_0_
  49.0 0.0 collective-permute-start.6
  49.0 0.8 shard_map.133
  49.8 0.0 copy-done.2
  49.8 1.5 %shard_map.136.known_ref = f32[64,4,128]{2,1,0:T(4,128)S(1)} custom-call(f32[2,2048]{1,0:T(2,128)S(1)} %fusion.moved_ref, s32[1,2048]{1,0:T(1,128)S(1)} %bitcast.10, s32[1,2048]{1,0:T(1,128)S(1)} %get-tuple-element.61.code_ref, f32[3,2048]{1,0:T(4,128)S(1)} %copy-done.2), custom_call_target="tpu_custom_call" | custom-call | tf_op jit(solution)/shard_map/pallas_call | solution.py:437
  51.3 0.0 collective-permute-done.2.refs_1_
  51.3 0.0 collective-permute-done.3.refs_2_
  51.3 0.0 collective-permute-done.4.refs_3_
  51.3 0.0 collective-permute-done.5.refs_4_
  51.3 2.6 %collective-permute-done.6.refs_5_ = f32[16,256]{1,0:T(8,128)S(1)} collective-permute-done((f32[16,256]{1,0:T(8,128)S(1)}, f32[16,256]{1,0:T(8,128)S(1)}, u32[]{:S(2)}, u32[]{:S(2)}) %collective-permute-start.6) | collective-permute-done | bytes 16416 | tf_op jit(solution)/shard_map/ppermute | solution.py:477
  53.9 2.8 %shard_map.135 = (f32[4,64,512]{2,1,0:T(8,128)S(1)}, f32[6,64,256]{2,1,0:T(8,128)S(1)}, f32[16,256]{1,0:T(8,128)S(1)}, f32[16,256]{1,0:T(8,128)S(1)}, f32[16,256...) custom-call(f32[4,64,512]{2,1,0:T(8,128)} %state_ref.5, ...), custom_call_target="tpu_custom_call" | custom-call | tf_op jit(solution)/shard_map/pallas_call | solution.py:437
  56.8 0.0 all-to-all-done.1.back_ref
  56.8 1.3 %shard_map.137 = f32[64,4,128]{2,1,0:T(4,128)S(1)} custom-call(s32[1]{0:T(128)} %copy.14.cut_ref, f32[64,4,128]{2,1,0:T(4,128)S(1)} %all-to-all-done.1.back_ref, f32[2,2048]{1,0:T(2,128)S(1)} %fusion.moved_ref, f32[64,4,128]{2,1,0:T(4,128)S(1)} %shard_map.136.known_ref, s32[1,2048]{1,0:T(1,128)S(1)} %get-tuple-element.61.code_ref), custom_call_target="tpu_custom_call" | custom-call | tf_op jit(solution)/shard_map/pallas_call | solution.py:437
  58.1 15.8 %all_to_all.20.incoming_ref = f32[64,4,128]{2,1,0:T(4,128)S(1)} all-to-all(f32[64,4,128]{2,1,0:T(4,128)S(1)} %shard_map.137), channel_id=1, replica_groups=mesh['gx'=4,'gy'=8,'gz'=8] {'gy','gz'}, dimensions={0} | all-to-all | bytes 262144 | tf_op jit(solution)/shard_map/all_to_all | solution.py:469
  73.8 6.5 %shard_map.138 = (f32[64,2,128]{2,1,0:T(2,128)}, f32[256,512]{1,0:T(8,128)S(1)}) custom-call(f32[64,4,128]{2,1,0:T(4,128)S(1)} %all_to_all.20.incoming_ref, f32[4,64,512]{2,1,0:T(8,128)S(1)} %get-tuple-element.68.state_ref), custom_call_target="tpu_custom_call" | custom-call | tf_op jit(solution)/shard_map/pallas_call | solution.py:437
  80.3 7.0 %all-to-all-start.3 = ((f32[64,2,128]{2,1,0:T(2,128)}), f32[64,2,128]{2,1,0:T(2,128)S(1)}, u32[]{:S(2)}, u32[]{:S(2)}) async-start(f32[64,2,128]{2,1,0:T(2,128)} %get-tuple-element.79), calls=%async_computation.3 | async-start | bytes 131072 | tf_op jit(solution)/shard_map/all_to_all | solution.py:469
  87.3 0.4 collective-permute-start.7
  87.7 2.9 %collective-permute-start.8 = (f32[16,256]{1,0:T(8,128)S(1)}, f32[16,256]{1,0:T(8,128)S(1)}, u32[]{:S(2)}, u32[]{:S(2)}) collective-permute-start(f32[16,256]{1,0:T(8,128)S(1)} %get-tuple-element.74), channel_id=1, source_target_pairs={{64,0},{128,64},{192,128},{0,192},{65,1},{129,65},{193,129},{1,193... | collective-permute-start | bytes 49160 | tf_op jit(solution)/shard_map/ppermute | solution.py:477
  90.6 0.0 collective-permute-start.9
  90.6 3.0 %collective-permute-start.10 = (f32[16,256]{1,0:T(8,128)S(1)}, f32[16,256]{1,0:T(8,128)S(1)}, u32[]{:S(2)}, u32[]{:S(2)}) collective-permute-start(f32[16,256]{1,0:T(8,128)S(1)} %get-tuple-element.76), channel_id=1, source_target_pairs={{8,0},{16,8},{24,16},{32,24},{40,32},{48,40},{56,48},{0,56},{9,1},... | collective-permute-start | bytes 49160 | tf_op jit(solution)/shard_map/ppermute | solution.py:477
  93.5 2.7 %collective-permute-start.11 = (f32[16,256]{1,0:T(8,128)S(1)}, f32[16,256]{1,0:T(8,128)S(1)}, u32[]{:S(2)}, u32[]{:S(2)}) collective-permute-start(f32[16,256]{1,0:T(8,128)S(1)} %get-tuple-element.77), channel_id=1, source_target_pairs={{0,1},{1,2},{2,3},{3,4},{4,5},{5,6},{6,7},{7,0},{8,9},{9,10},{10,1... | collective-permute-start | bytes 49160 | tf_op jit(solution)/shard_map/ppermute | solution.py:476
  96.2 0.0 collective-permute-done.7.refs_0_
  96.2 0.0 collective-permute-start.12
  96.2 0.0 collective-permute-done.8.refs_1_
  96.2 0.0 collective-permute-done.9.refs_2_
  96.2 0.0 collective-permute-done.10.refs_3_
  96.3 1.4 %collective-permute-done.11.refs_4_ = f32[16,256]{1,0:T(8,128)S(1)} collective-permute-done((f32[16,256]{1,0:T(8,128)S(1)}, f32[16,256]{1,0:T(8,128)S(1)}, u32[]{:S(2)}, u32[]{:S(2)}) %collective-permute-start.11) | collective-permute-done | bytes 16416 | tf_op jit(solution)/shard_map/ppermute | solution.py:476
  97.7 3.5 %collective-permute-done.12.refs_5_ = f32[16,256]{1,0:T(8,128)S(1)} collective-permute-done((f32[16,256]{1,0:T(8,128)S(1)}, f32[16,256]{1,0:T(8,128)S(1)}, u32[]{:S(2)}, u32[]{:S(2)}) %collective-permute-start.12) | collective-permute-done | bytes 16416 | tf_op jit(solution)/shard_map/ppermute | solution.py:477
  101.2 2.8 %shard_map.139 = f32[4,64,512]{2,1,0:T(8,128)} custom-call(f32[4,64,512]{2,1,0:T(8,128)S(1)} %get-tuple-element.68.state_ref, f32[256,512]{1,0:T(8,128)S(1)} %get-tuple-element.71.force_ref, bf16[6,64,128]{2,1,0:T(8,128)(2,1)S(1)} %get-tuple-element.49.own_ref, bf16[6,64,32]{2,1,0:T(8,128)(2,1)S(1)} %get-tuple-element.50.far_ref, ...), custom_call_target="tpu_custom_call" | custom-call | tf_op jit(solution)/shard_map/pallas_call | solution.py:437
  104.0 0.0 all-to-all-done.3.back_ref
  104.0 1.1 %shard_map.140 = f32[3,2048]{1,0:T(4,128)} custom-call(f32[64,2,128]{2,1,0:T(2,128)S(1)} %all-to-all-done.3.back_ref, s32[1,2048]{1,0:T(1,128)S(1)} %get-tuple-element.61.code_ref), custom_call_target="tpu_custom_call" | custom-call | tf_op jit(solution)/shard_map/pallas_call | solution.py:437
  (6 shorter events, 0.0 us)
Async XLA Ops:
  3.9 10.8 %copy-start.4 = (f32[2,2048]{1,0:T(2,128)S(1)}, f32[2,2048]{1,0:T(2,128)}, u32[]{:S(2)}) copy-start(f32[2,2048]{1,0:T(2,128)} %get-tuple-element.42) | copy-start | bytes 49156
  3.9 19.8 %all-to-all-start = ((f32[64,4,128]{2,1,0:T(4,128)}), f32[64,4,128]{2,1,0:T(4,128)S(1)}, u32[]{:S(2)}, u32[]{:S(2)}) async-start(f32[64,4,128]{2,1,0:T(4,128)} %get-tuple-element.41), calls=%async_computation | async-start | bytes 262144 | tf_op jit(solution)/shard_map/all_to_all | solution.py:469
  14.7 6.6 %collective-permute-start = (f32[2,2048]{1,0:T(2,128)S(1)}, f32[2,2048]{1,0:T(2,128)S(1)}, u32[]{:S(2)}, u32[]{:S(2)}) collective-permute-start(f32[2,2048]{1,0:T(2,128)S(1)} %copy-done.4), channel_id=1, source_target_pairs={{1,0},{2,1},{3,2},{4,3},{5,4},{6,5},{7,6},{8,7},{9,8},{10,9},{11,1... | collective-permute-start | bytes 49160 | tf_op jit(solution)/shard_map/ppermute | solution.py:507
  23.7 1.0 copy-start
  31.2 25.6 %all-to-all-start.1 = ((f32[64,4,128]{2,1,0:T(4,128)}), f32[64,4,128]{2,1,0:T(4,128)S(1)}, u32[]{:S(2)}, u32[]{:S(2)}) async-start(f32[64,4,128]{2,1,0:T(4,128)} %get-tuple-element.44), calls=%async_computation.1 | async-start | bytes 262144 | tf_op jit(solution)/shard_map/all_to_all | solution.py:469
  37.9 12.0 %copy-start.2 = (f32[3,2048]{1,0:T(4,128)S(1)}, f32[3,2048]{1,0:T(4,128)}, u32[]{:S(2)}) copy-start(f32[3,2048]{1,0:T(4,128)} %coord_ref.3) | copy-start | bytes 73732
  40.1 8.9 %copy-start.1 = (s32[2048]{0:T(1024)S(1)}, s32[2048]{0:T(1024)}, u32[]{:S(2)}) copy-start(s32[2048]{0:T(1024)} %param.16) | copy-start | bytes 24580
  40.1 8.9 %collective-permute-start.1 = (f32[16,256]{1,0:T(8,128)S(1)}, f32[16,256]{1,0:T(8,128)S(1)}, u32[]{:S(2)}, u32[]{:S(2)}) collective-permute-start(f32[16,256]{1,0:T(8,128)S(1)} %get-tuple-element.52), channel_id=1, source_target_pairs={{0,64},{64,128},{128,192},{192,0},{1,65},{65,129},{129,193},{193,1... | collective-permute-start | bytes 49160 | tf_op jit(solution)/shard_map/ppermute | solution.py:476
  41.7 9.6 %collective-permute-start.2 = (f32[16,256]{1,0:T(8,128)S(1)}, f32[16,256]{1,0:T(8,128)S(1)}, u32[]{:S(2)}, u32[]{:S(2)}) collective-permute-start(f32[16,256]{1,0:T(8,128)S(1)} %get-tuple-element.53), channel_id=1, source_target_pairs={{64,0},{128,64},{192,128},{0,192},{65,1},{129,65},{193,129},{1,193... | collective-permute-start | bytes 49160 | tf_op jit(solution)/shard_map/ppermute | solution.py:477
  43.3 8.0 %collective-permute-start.3 = (f32[16,256]{1,0:T(8,128)S(1)}, f32[16,256]{1,0:T(8,128)S(1)}, u32[]{:S(2)}, u32[]{:S(2)}) collective-permute-start(f32[16,256]{1,0:T(8,128)S(1)} %get-tuple-element.54), channel_id=1, source_target_pairs={{0,8},{8,16},{16,24},{24,32},{32,40},{40,48},{48,56},{56,0},{1,9},... | collective-permute-start | bytes 49160 | tf_op jit(solution)/shard_map/ppermute | solution.py:476
  43.3 5.6 %copy-start.3 = (s32[64,6]{0,1:T(8,128)S(1)}, s32[64,6]{0,1:T(8,128)}, u32[]{:S(2)}) copy-start(s32[64,6]{0,1:T(8,128)} %param.13) | copy-start | bytes 4612
  43.3 8.0 %collective-permute-start.4 = (f32[16,256]{1,0:T(8,128)S(1)}, f32[16,256]{1,0:T(8,128)S(1)}, u32[]{:S(2)}, u32[]{:S(2)}) collective-permute-start(f32[16,256]{1,0:T(8,128)S(1)} %get-tuple-element.55), channel_id=1, source_target_pairs={{8,0},{16,8},{24,16},{32,24},{40,32},{48,40},{56,48},{0,56},{9,1},... | collective-permute-start | bytes 49160 | tf_op jit(solution)/shard_map/ppermute | solution.py:477
  46.3 5.0 %collective-permute-start.5 = (f32[16,256]{1,0:T(8,128)S(1)}, f32[16,256]{1,0:T(8,128)S(1)}, u32[]{:S(2)}, u32[]{:S(2)}) collective-permute-start(f32[16,256]{1,0:T(8,128)S(1)} %get-tuple-element.56), channel_id=1, source_target_pairs={{0,1},{1,2},{2,3},{3,4},{4,5},{5,6},{6,7},{7,0},{8,9},{9,10},{10,1... | collective-permute-start | bytes 49160 | tf_op jit(solution)/shard_map/ppermute | solution.py:476
  49.0 5.0 %collective-permute-start.6 = (f32[16,256]{1,0:T(8,128)S(1)}, f32[16,256]{1,0:T(8,128)S(1)}, u32[]{:S(2)}, u32[]{:S(2)}) collective-permute-start(f32[16,256]{1,0:T(8,128)S(1)} %get-tuple-element.57), channel_id=1, source_target_pairs={{1,0},{2,1},{3,2},{4,3},{5,4},{6,5},{7,6},{0,7},{9,8},{10,9},{11,1... | collective-permute-start | bytes 49160 | tf_op jit(solution)/shard_map/ppermute | solution.py:477
  80.3 23.7 %all-to-all-start.3 = ((f32[64,2,128]{2,1,0:T(2,128)}), f32[64,2,128]{2,1,0:T(2,128)S(1)}, u32[]{:S(2)}, u32[]{:S(2)}) async-start(f32[64,2,128]{2,1,0:T(2,128)} %get-tuple-element.79), calls=%async_computation.3 | async-start | bytes 131072 | tf_op jit(solution)/shard_map/all_to_all | solution.py:469
  87.3 9.0 %collective-permute-start.7 = (f32[16,256]{1,0:T(8,128)S(1)}, f32[16,256]{1,0:T(8,128)S(1)}, u32[]{:S(2)}, u32[]{:S(2)}) collective-permute-start(f32[16,256]{1,0:T(8,128)S(1)} %get-tuple-element.73), channel_id=1, source_target_pairs={{0,64},{64,128},{128,192},{192,0},{1,65},{65,129},{129,193},{193,1... | collective-permute-start | bytes 49160 | tf_op jit(solution)/shard_map/ppermute | solution.py:476
  87.7 8.5 %collective-permute-start.8 = (f32[16,256]{1,0:T(8,128)S(1)}, f32[16,256]{1,0:T(8,128)S(1)}, u32[]{:S(2)}, u32[]{:S(2)}) collective-permute-start(f32[16,256]{1,0:T(8,128)S(1)} %get-tuple-element.74), channel_id=1, source_target_pairs={{64,0},{128,64},{192,128},{0,192},{65,1},{129,65},{193,129},{1,193... | collective-permute-start | bytes 49160 | tf_op jit(solution)/shard_map/ppermute | solution.py:477
  90.6 5.7 %collective-permute-start.9 = (f32[16,256]{1,0:T(8,128)S(1)}, f32[16,256]{1,0:T(8,128)S(1)}, u32[]{:S(2)}, u32[]{:S(2)}) collective-permute-start(f32[16,256]{1,0:T(8,128)S(1)} %get-tuple-element.75), channel_id=1, source_target_pairs={{0,8},{8,16},{16,24},{24,32},{32,40},{40,48},{48,56},{56,0},{1,9},... | collective-permute-start | bytes 49160 | tf_op jit(solution)/shard_map/ppermute | solution.py:476
  90.6 5.7 %collective-permute-start.10 = (f32[16,256]{1,0:T(8,128)S(1)}, f32[16,256]{1,0:T(8,128)S(1)}, u32[]{:S(2)}, u32[]{:S(2)}) collective-permute-start(f32[16,256]{1,0:T(8,128)S(1)} %get-tuple-element.76), channel_id=1, source_target_pairs={{8,0},{16,8},{24,16},{32,24},{40,32},{48,40},{56,48},{0,56},{9,1},... | collective-permute-start | bytes 49160 | tf_op jit(solution)/shard_map/ppermute | solution.py:477
  93.5 4.1 %collective-permute-start.11 = (f32[16,256]{1,0:T(8,128)S(1)}, f32[16,256]{1,0:T(8,128)S(1)}, u32[]{:S(2)}, u32[]{:S(2)}) collective-permute-start(f32[16,256]{1,0:T(8,128)S(1)} %get-tuple-element.77), channel_id=1, source_target_pairs={{0,1},{1,2},{2,3},{3,4},{4,5},{5,6},{6,7},{7,0},{8,9},{9,10},{10,1... | collective-permute-start | bytes 49160 | tf_op jit(solution)/shard_map/ppermute | solution.py:476
  96.2 5.0 %collective-permute-start.12 = (f32[16,256]{1,0:T(8,128)S(1)}, f32[16,256]{1,0:T(8,128)S(1)}, u32[]{:S(2)}, u32[]{:S(2)}) collective-permute-start(f32[16,256]{1,0:T(8,128)S(1)} %get-tuple-element.78), channel_id=1, source_target_pairs={{1,0},{2,1},{3,2},{4,3},{5,4},{6,5},{7,6},{0,7},{9,8},{10,9},{11,1... | collective-permute-start | bytes 49160 | tf_op jit(solution)/shard_map/ppermute | solution.py:477
